TPU v7x, 128 devices: a whole 4x4x4 slice. The times are simulated.
128 devices in a mesh: row: 16 (over y, z), col: 8 (over x, core).
Axes of the slice: x: 4, y: 4, z: 4, core: 2. Of those that a mesh axis runs over, the one named last changes fastest.
Arguments:
- points: bfloat16 [64, 262144], P(None, ('row', 'col')), may hold values from -6 to 6
- weights: float32 [16, 262144], P(None, ('row', 'col')), may hold values from -1.2 to 1.2
- targets: float32 [16, 262144], P(None, ('row', 'col')), may hold values from -6 to 6
- block_index: int32 [1, 16384], replicated, may hold values from 0 to 262143, as said below
Outputs:
- weights_out: float32 [16, 262144], P(None, ('row', 'col'))
- residual: float32 [16, 16384], P(None, ('row', 'col'))
Inputs may be any that keep to these rules, and one draw needn't show every extreme that they name: `block_index`: each row is increasing. Point p is held by the device of flat index p // 2048 (row index first). Each aligned run of 2048 points holds at most 256 entries of a row, and some run exactly 256; each aligned run of 16384 points holds exactly 1024 entries of a row.
All inputs are finite; a program needn't handle non-finite values.
Results may differ from a plain program's by a relative error of at most 0.028.
Values may be sent and summed in bfloat16 or wider, within the bound.
A program may use at most 64 MiB of HBM per device.

v0:
```python
import jax
import jax.numpy as jnp
from jax import lax
from jax.sharding import Mesh
from jax.sharding import PartitionSpec as P

RANK = 256
CG_ITERS = 2
ROW = ("row_0", "row_1")
COL = ("col_0", "col_1")
ROW_COL = ("row_0", "row_1", "col_0", "col_1")


ridge = 1.0
piece_limit = 2048


def in_order(parts, dim):
    parts = jnp.moveaxis(parts, 0, dim)
    lengths = parts.shape
    return parts.reshape(*lengths[:dim], lengths[dim] * lengths[dim + 1], *lengths[dim + 2 :])


def copy_for_each(array, axis):
    devices = lax.axis_size(axis)
    return lax.all_to_all(
        jnp.broadcast_to(array[None], (devices, *array.shape)), axis, 0, 0, tiled=True
    )


def gather_directly(array, axis, dim):
    return in_order(copy_for_each(array, axis), dim)


def cut_along(array, dim, devices):
    lengths = array.shape
    parts = array.reshape(*lengths[:dim], devices, lengths[dim] // devices, *lengths[dim + 1 :])
    return jnp.moveaxis(parts, dim, 0)


def sum_at_owner(array, axis, dim):
    parts = cut_along(array, dim, lax.axis_size(axis))
    arrived = lax.all_to_all(parts, axis, split_axis=0, concat_axis=0, tiled=True)
    return arrived.sum(axis=0)


def sum_by_axis(array, axes, dim):
    far, near = axes
    own = sum_at_owner(cut_along(array, dim, lax.axis_size(far)), near, dim + 1)
    return jnp.sum(lax.all_to_all(own, far, 0, 0, tiled=True), axis=0)


def rows_for(lines, devices):
    spare = -lines.shape[0] % devices
    if not spare:
        return lines
    return jnp.concatenate([lines, jnp.zeros((spare, *lines.shape[1:]), lines.dtype)])


def gather_axes(array, axes, dim):
    far, near = axes
    parts = copy_for_each(copy_for_each(array, far), near)
    return in_order(parts.swapaxes(0, 1).reshape(-1, *array.shape), dim)


def sum_by_parts(array, axes):
    lines = array.reshape(-1, array.shape[-1])
    padded = rows_for(lines, lax.axis_size(axes[0]) * lax.axis_size(axes[1]))
    whole = gather_axes(sum_by_axis(padded, axes, 0), axes, 0)
    return lax.slice_in_dim(whole, 0, len(lines)).reshape(array.shape)


def sum_at_owner_2(array, axis, dim):
    parts = cut_along(array, dim, lax.axis_size(axis))
    arrived = lax.all_to_all(parts, axis, split_axis=0, concat_axis=0, tiled=True)
    return arrived.astype(jnp.float32).sum(axis=0)


def taken_together(array, axis):
    everything = copy_for_each(array, axis)
    return jnp.sum(everything, axis=0)


def by_axis(array, axes):
    far, near = axes
    nearer = taken_together(array, near)
    return taken_together(nearer, far)


def packed_total(arrays, axis):
    ravelled, at, outs = (jnp.concatenate([a.reshape(-1) for a in arrays]), 0, [])
    so_far = by_axis(ravelled, axis)
    for a in arrays:
        outs.append(so_far[at : at + a.size].reshape(a.shape))
        at += a.size
    return tuple(outs)


def point_squares(points):
    values = points.astype(jnp.float32)
    return jnp.sum(values * values, axis=0)


def kernel_block(left, right, left_sq, right_sq):
    cross = lax.dot_general(
        left, right, (((0,), (0,)), ((), ())), preferred_element_type=jnp.float32
    )
    return jnp.exp(-(2.0 / left.shape[0]) * (left_sq[:, None] + right_sq[None, :] - 2.0 * cross))


def solve_inner(chol, projected):
    middle = lax.linalg.triangular_solve(chol, projected.T, left_side=True, lower=True)
    return lax.linalg.triangular_solve(chol, middle, left_side=True, lower=True, transpose_a=True).T


def on_device(points, weights, targets, block_index):
    features, owned = points.shape
    target_count = weights.shape[0]
    row_count = lax.axis_size(ROW)
    col_count = lax.axis_size(COL)
    devices = row_count * col_count
    row_index = lax.axis_index(ROW)
    col_index = lax.axis_index(COL)
    device = row_index * col_count + col_index
    block_len = block_index.shape[1]
    share = block_len // devices
    capacity = 2 * share
    row_len = block_len // row_count
    col_len = block_len // col_count
    first_point = device * owned
    own_squares = point_squares(points)
    owner_starts = jnp.arange(devices, dtype=jnp.int32) * owned
    weights_now = weights
    chosen = block_index[0]
    before = jnp.sum((chosen < first_point).astype(jnp.int32))
    count = jnp.sum((chosen < first_point + owned).astype(jnp.int32)) - before
    slots = jnp.arange(capacity, dtype=jnp.int32)
    valid = slots < count
    where_at = jnp.minimum(before + slots, block_len - 1)
    local = jnp.clip(chosen[where_at] - first_point, 0, owned - 1)
    mine = jnp.where(valid[None, :], points[:, local], jnp.zeros((), jnp.bfloat16))
    firsts = jnp.sum((chosen[None, :] < owner_starts[:, None]).astype(jnp.int32), axis=1)
    section = gather_directly(mine, COL, 1)
    rows_at = row_index * row_len + jnp.arange(row_len, dtype=jnp.int32)
    holder = chosen[rows_at] // owned
    placing = holder % col_count * capacity + rows_at - firsts[holder]
    compact = section[:, placing]
    block_pts = gather_directly(compact, ROW, 1)
    block_sq = point_squares(block_pts)
    weights_bf = weights_now.astype(jnp.bfloat16)
    span = min(block_len, piece_limit)

    def slab_piece(index, total):
        left = lax.dynamic_slice_in_dim(block_pts, index * span, span, 1)
        left_sq = lax.dynamic_slice_in_dim(block_sq, index * span, span, 0)
        kern = kernel_block(points, left, own_squares, left_sq).astype(jnp.bfloat16)
        part = jnp.dot(weights_bf, kern, preferred_element_type=jnp.float32)
        return lax.dynamic_update_slice_in_dim(total, part, index * span, 1)

    slab = lax.fori_loop(
        0, block_len // span, slab_piece, jnp.zeros((target_count, block_len), jnp.float32)
    )
    own_values = jnp.where(valid[None, :], targets[:, local] - ridge * weights_now[:, local], 0.0)
    padded = jnp.zeros((target_count, block_len + capacity), jnp.float32)
    padded = lax.dynamic_update_slice_in_dim(padded, own_values, before, 1)
    rhs = -sum_by_axis(slab - padded[:, :block_len], (("row_0", "row_1", "col_0"), "col_1"), 1)
    marks_pts = block_pts[:, :RANK]
    marks_sq = block_sq[:RANK]
    share_pts = lax.dynamic_slice_in_dim(block_pts, device * share, share, 1)
    share_sq = lax.dynamic_slice_in_dim(block_sq, device * share, share, 0)
    sketch = kernel_block(share_pts, marks_pts, share_sq, marks_sq)
    gram = sum_by_parts(
        jnp.dot(sketch.T, sketch, precision=lax.Precision.HIGHEST),
        (("row_0", "row_1", "col_0"), "col_1"),
    )
    inner = ridge * kernel_block(marks_pts, marks_pts, marks_sq, marks_sq) + gram
    chol = jnp.linalg.cholesky(inner)
    rows_pts = lax.dynamic_slice_in_dim(block_pts, row_index * row_len, row_len, 1)
    rows_sq = lax.dynamic_slice_in_dim(block_sq, row_index * row_len, row_len, 0)
    grid_pts = block_pts.reshape(features, row_count, col_count, share)
    cols_pts = lax.dynamic_index_in_dim(grid_pts, col_index, 2, keepdims=False).reshape(
        features, col_len
    )
    grid_sq = block_sq.reshape(row_count, col_count, share)
    cols_sq = lax.dynamic_index_in_dim(grid_sq, col_index, 1, keepdims=False).reshape(col_len)
    tile = kernel_block(rows_pts, cols_pts, rows_sq, cols_sq).astype(jnp.bfloat16)

    def precondition(vector):
        projected, norms = packed_total(
            (
                jnp.dot(vector, sketch, precision=lax.Precision.HIGHEST),
                jnp.sum(vector * vector, axis=1),
            ),
            (("row_0", "row_1"), ("col_0", "col_1")),
        )
        solved = solve_inner(chol, projected)
        result = (vector - jnp.dot(solved, sketch.T, precision=lax.Precision.HIGHEST)) / ridge
        return (result, (norms - jnp.sum(projected * solved, axis=1)) / ridge)

    residual = rhs
    delta = jnp.zeros((target_count, share), jnp.float32)
    precond, inner_rz = precondition(residual)
    direction = precond
    for turn in range(CG_ITERS):
        partial_sum = lax.dot_general(
            gather_directly(direction.astype(jnp.bfloat16), ROW, 1),
            tile,
            (((1,), (1,)), ((), ())),
            preferred_element_type=jnp.float32,
        )
        image = sum_at_owner_2(partial_sum.astype(jnp.bfloat16), COL, 1) + ridge * direction
        curve = by_axis(jnp.sum(direction * image, axis=1), (("row_0", "row_1", "col_0"), "col_1"))
        alpha = inner_rz / curve
        delta = delta + alpha[:, None] * direction
        residual = residual - alpha[:, None] * image
        if turn + 1 < CG_ITERS:
            precond, fresh = precondition(residual)
            direction = precond + (fresh / inner_rz)[:, None] * direction
            inner_rz = fresh
    row_delta = gather_directly(delta, COL, 1)
    padded_delta = jnp.concatenate(
        [row_delta, jnp.zeros((target_count, capacity), jnp.float32)], axis=1
    )
    offset = jnp.clip(before - row_index * row_len, 0, row_len)
    own_delta = jnp.where(
        valid[None, :], lax.dynamic_slice_in_dim(padded_delta, offset, capacity, 1), 0.0
    )
    selector = (
        (local[:, None] == jnp.arange(owned, dtype=jnp.int32)[None, :]) & valid[:, None]
    ).astype(jnp.float32)
    weights_now = weights_now + jnp.dot(own_delta, selector, precision=lax.Precision.HIGHEST)
    return (weights_now, residual)


def solution(mesh):
    split = Mesh(mesh.devices.reshape(4, 4, 4, 2), ("row_0", "row_1", "col_0", "col_1"))
    return jax.shard_map(
        on_device,
        mesh=split,
        in_specs=(P(None, ROW_COL), P(None, ROW_COL), P(None, ROW_COL), P()),
        out_specs=(P(None, ROW_COL), P(None, ROW_COL)),
        check_vma=False,
    )
```

profile of v0, /device:TPU:1, one launch (start us, length us, event | category | flops | bytes accessed | tf_op | source)
XLA Modules:
  0.0 400.9 jit_solution(13259356118574827837)
XLA Ops:
  34.8 8.1 %all-to-all-start.1 = ((bf16[16,64,1024]{2,1,0:T(8,128)(2,1)}), bf16[16,64,1024]{2,1,0:T(8,128)(2,1)S(1)}, u32[]{:S(2)}, u32[]{:S(2)}) async-start(bf16[16,64,1024]{2,1,0:T(8,128)(2,1)} %broadcast_in_dim.75), calls=%async_computation.1 | async-start | bytes 4194304 | tf_op jit(solution)/shard_map/all_to_all | solution.py:26
  56.1 15.8 %all-to-all-done.1 = bf16[16,64,1024]{2,1,0:T(8,128)(2,1)S(1)} async-done(((bf16[16,64,1024]{2,1,0:T(8,128)(2,1)}), bf16[16,64,1024]{2,1,0:T(8,128)(2,1)S(1)}, u32[]{:S(2)}, u32[]{:S(2)}) %all-to-all-start.1) | async-done | bytes 2097184 | tf_op jit(solution)/shard_map/all_to_all | solution.py:26
  76.2 55.7 %while.21 = (s32[]{:T(128)}, f32[16,16384]{1,0:T(8,128)}, f32[2048]{0:T(1024)S(1)}, f32[16384]{0:T(1024)S(1)}, bf16[64,16384]{1,0:T(8,128)(2,1)}, /*index=5*/bf1...) while((s32[]{:T(128)}, f32[16,16384]{1,0:T(8,128)}, ...), condition=%wide.region_6.7_spmd, body=%wide.region_5.6_spmd.sunk | while | flops 692060160 | bytes 754847 | solution.py:160
  76.2 7.0 %fusion.113 = f32[16,16384]{1,0:T(8,128)} fusion(f32[16,16384]{1,0:T(8,128)} %get-tuple-element.308, s32[]{:T(128)S(6)} %select_n.167, bf16[16,2048]{1,0:T(8,128)(2,1)} %get-tuple-element.324, bf16[64,2048]{1,0:T(8,128)(2,1)S(1)} %get-tuple-element.323, f32[2048]{0:T(1024)S(1)} %dynamic_slice.60, f32[2048]{0:T(1024)S(1)} %get-tuple-element.320, ...), kind=kOutput, calls=%fused_computation.13.clone.1 | convolution fusion | flops 692060160 | bytes 738304 | tf_op jit(solution)/shard_map/while/body/eval_jaxpr/dot_general | solution.py:157
  83.2 6.9 %fusion.113 = f32[16,16384]{1,0:T(8,128)} fusion(f32[16,16384]{1,0:T(8,128)} %get-tuple-element.308, s32[]{:T(128)S(6)} %select_n.167, bf16[16,2048]{1,0:T(8,128)(2,1)} %get-tuple-element.324, bf16[64,2048]{1,0:T(8,128)(2,1)S(1)} %get-tuple-element.323, f32[2048]{0:T(1024)S(1)} %dynamic_slice.60, f32[2048]{0:T(1024)S(1)} %get-tuple-element.320, ...), kind=kOutput, calls=%fused_computation.13.clone.1 | convolution fusion | flops 692060160 | bytes 738304 | tf_op jit(solution)/shard_map/while/body/eval_jaxpr/dot_general | solution.py:157
  90.2 7.0 %fusion.113 = f32[16,16384]{1,0:T(8,128)} fusion(f32[16,16384]{1,0:T(8,128)} %get-tuple-element.308, s32[]{:T(128)S(6)} %select_n.167, bf16[16,2048]{1,0:T(8,128)(2,1)} %get-tuple-element.324, bf16[64,2048]{1,0:T(8,128)(2,1)S(1)} %get-tuple-element.323, f32[2048]{0:T(1024)S(1)} %dynamic_slice.60, f32[2048]{0:T(1024)S(1)} %get-tuple-element.320, ...), kind=kOutput, calls=%fused_computation.13.clone.1 | convolution fusion | flops 692060160 | bytes 738304 | tf_op jit(solution)/shard_map/while/body/eval_jaxpr/dot_general | solution.py:157
  97.1 7.0 %fusion.113 = f32[16,16384]{1,0:T(8,128)} fusion(f32[16,16384]{1,0:T(8,128)} %get-tuple-element.308, s32[]{:T(128)S(6)} %select_n.167, bf16[16,2048]{1,0:T(8,128)(2,1)} %get-tuple-element.324, bf16[64,2048]{1,0:T(8,128)(2,1)S(1)} %get-tuple-element.323, f32[2048]{0:T(1024)S(1)} %dynamic_slice.60, f32[2048]{0:T(1024)S(1)} %get-tuple-element.320, ...), kind=kOutput, calls=%fused_computation.13.clone.1 | convolution fusion | flops 692060160 | bytes 738304 | tf_op jit(solution)/shard_map/while/body/eval_jaxpr/dot_general | solution.py:157
  104.1 7.0 %fusion.113 = f32[16,16384]{1,0:T(8,128)} fusion(f32[16,16384]{1,0:T(8,128)} %get-tuple-element.308, s32[]{:T(128)S(6)} %select_n.167, bf16[16,2048]{1,0:T(8,128)(2,1)} %get-tuple-element.324, bf16[64,2048]{1,0:T(8,128)(2,1)S(1)} %get-tuple-element.323, f32[2048]{0:T(1024)S(1)} %dynamic_slice.60, f32[2048]{0:T(1024)S(1)} %get-tuple-element.320, ...), kind=kOutput, calls=%fused_computation.13.clone.1 | convolution fusion | flops 692060160 | bytes 738304 | tf_op jit(solution)/shard_map/while/body/eval_jaxpr/dot_general | solution.py:157
  111.1 7.0 %fusion.113 = f32[16,16384]{1,0:T(8,128)} fusion(f32[16,16384]{1,0:T(8,128)} %get-tuple-element.308, s32[]{:T(128)S(6)} %select_n.167, bf16[16,2048]{1,0:T(8,128)(2,1)} %get-tuple-element.324, bf16[64,2048]{1,0:T(8,128)(2,1)S(1)} %get-tuple-element.323, f32[2048]{0:T(1024)S(1)} %dynamic_slice.60, f32[2048]{0:T(1024)S(1)} %get-tuple-element.320, ...), kind=kOutput, calls=%fused_computation.13.clone.1 | convolution fusion | flops 692060160 | bytes 738304 | tf_op jit(solution)/shard_map/while/body/eval_jaxpr/dot_general | solution.py:157
  118.0 7.0 %fusion.113 = f32[16,16384]{1,0:T(8,128)} fusion(f32[16,16384]{1,0:T(8,128)} %get-tuple-element.308, s32[]{:T(128)S(6)} %select_n.167, bf16[16,2048]{1,0:T(8,128)(2,1)} %get-tuple-element.324, bf16[64,2048]{1,0:T(8,128)(2,1)S(1)} %get-tuple-element.323, f32[2048]{0:T(1024)S(1)} %dynamic_slice.60, f32[2048]{0:T(1024)S(1)} %get-tuple-element.320, ...), kind=kOutput, calls=%fused_computation.13.clone.1 | convolution fusion | flops 692060160 | bytes 738304 | tf_op jit(solution)/shard_map/while/body/eval_jaxpr/dot_general | solution.py:157
  125.0 7.0 %fusion.113 = f32[16,16384]{1,0:T(8,128)} fusion(f32[16,16384]{1,0:T(8,128)} %get-tuple-element.308, s32[]{:T(128)S(6)} %select_n.167, bf16[16,2048]{1,0:T(8,128)(2,1)} %get-tuple-element.324, bf16[64,2048]{1,0:T(8,128)(2,1)S(1)} %get-tuple-element.323, f32[2048]{0:T(1024)S(1)} %dynamic_slice.60, f32[2048]{0:T(1024)S(1)} %get-tuple-element.320, ...), kind=kOutput, calls=%fused_computation.13.clone.1 | convolution fusion | flops 692060160 | bytes 738304 | tf_op jit(solution)/shard_map/while/body/eval_jaxpr/dot_general | solution.py:157
  142.2 7.6 %all-to-all-start.7 = ((f32[64,2,256]{2,1,0:T(2,128)}), f32[64,2,256]{2,1,0:T(2,128)S(1)}, u32[]{:S(2)}, u32[]{:S(2)}) async-start(f32[64,2,256]{2,1,0:T(2,128)} %reduce_sum.238), calls=%async_computation.7 | async-start | bytes 262144 | tf_op jit(solution)/shard_map/all_to_all | solution.py:50
  166.4 7.9 %all-to-all-start.8 = ((f32[64,2,256]{2,1,0:T(2,128)}), f32[64,2,256]{2,1,0:T(2,128)S(1)}, u32[]{:S(2)}, u32[]{:S(2)}) async-start(f32[64,2,256]{2,1,0:T(2,128)} %broadcast_in_dim.80), calls=%async_computation.8 | async-start | bytes 262144 | tf_op jit(solution)/shard_map/all_to_all | solution.py:26
  195.7 11.7 %cholesky.50 = f32[128,128]{1,0:T(8,128)S(1)} custom-call(f32[128,128]{1,0:T(8,128)S(1)} %cholesky.118), custom_call_target="Cholesky" | custom-call | tf_op jit(solution)/shard_map/jit(cholesky)/cholesky | solution.py:177
  207.5 9.8 %custom-call.17 = f32[1,128,128]{1,2,0:T(8,128)S(1)} custom-call(f32[1,128,128]{2,1,0:T(8,128)S(1)} %get-tuple-element.198), custom_call_target="InvertDiagBlocksLowerTriangular" | custom-call | tf_op jit(solution)/shard_map/jit(cholesky)/cholesky | solution.py:177
  217.8 11.7 %cholesky.105 = f32[128,128]{1,0:T(8,128)S(1)} custom-call(f32[128,128]{1,0:T(8,128)S(1)} %convolution_subtract_fusion), custom_call_target="Cholesky" | custom-call | tf_op jit(solution)/shard_map/jit(cholesky)/cholesky | solution.py:177
  255.9 20.5 %custom-call.21 = f32[2,128,128]{1,2,0:T(8,128)S(1)} custom-call(f32[2,128,128]{2,1,0:T(8,128)} %get-tuple-element.158), custom_call_target="InvertDiagBlocksLowerTriangular" | custom-call | tf_op jit(solution)/shard_map/triangular_solve/custom-call.4 | solution.py:113
  295.4 10.1 %all_to_all.115 = bf16[8,16,128]{2,1,0:T(8,128)(2,1)S(1)} all-to-all(bf16[8,16,128]{2,1,0:T(8,128)(2,1)S(1)} %bitcast.227), channel_id=1, replica_groups=mesh['row_0'=4,'row_1'=4,'col_0'=4,'col_1'=2] {'col_0','col_1'}, dimensions={0} | all-to-all | bytes 65536 | tf_op jit(solution)/shard_map/all_to_all | solution.py:75
  316.2 8.2 %all-to-all-done.13 = f32[64,1,16]{2,1,0:T(1,128)S(1)} async-done(((f32[64,1,16]{2,1,0:T(1,128)}), f32[64,1,16]{2,1,0:T(1,128)S(1)}, u32[]{:S(2)}, u32[]{:S(2)}) %all-to-all-start.13) | async-done | bytes 4128 | tf_op jit(solution)/shard_map/all_to_all | solution.py:26
  325.0 9.4 %all_to_all.117 = f32[8,1,4112]{2,1,0:T(1,128)S(1)} all-to-all(f32[8,1,4112]{2,1,0:T(1,128)S(1)} %broadcast_in_dim.85), channel_id=1, replica_groups=mesh['row_0'=4,'row_1'=4,'col_0'=4,'col_1'=2] {'col_0','col_1'}, dimensions={0} | all-to-all | bytes 263168 | tf_op jit(solution)/shard_map/all_to_all | solution.py:26
  334.7 10.3 %all_to_all.118 = f32[16,1,4112]{2,1,0:T(1,128)S(1)} all-to-all(f32[16,1,4112]{2,1,0:T(1,128)S(1)} %broadcast_in_dim.86), channel_id=1, replica_groups=mesh['row_0'=4,'row_1'=4,'col_0'=4,'col_1'=2] {'row_0','row_1'}, dimensions={0} | all-to-all | bytes 526336 | tf_op jit(solution)/shard_map/all_to_all | solution.py:26
  346.8 10.0 %all_to_all.119 = bf16[16,16,128]{2,1,0:T(8,128)(2,1)S(1)} all-to-all(bf16[16,16,128]{2,1,0:T(8,128)(2,1)S(1)} %broadcast_in_dim.87), channel_id=1, replica_groups=mesh['row_0'=4,'row_1'=4,'col_0'=4,'col_1'=2] {'row_0','row_1'}, dimensions={0} | all-to-all | bytes 131072 | tf_op jit(solution)/shard_map/all_to_all | solution.py:26
  360.2 10.5 %all_to_all.120 = bf16[8,16,128]{2,1,0:T(8,128)(2,1)S(1)} all-to-all(bf16[8,16,128]{2,1,0:T(8,128)(2,1)S(1)} %bitcast.228), channel_id=1, replica_groups=mesh['row_0'=4,'row_1'=4,'col_0'=4,'col_1'=2] {'col_0','col_1'}, dimensions={0} | all-to-all | bytes 65536 | tf_op jit(solution)/shard_map/all_to_all | solution.py:75
  374.9 12.9 %all_to_all.122 = f32[64,1,16]{2,1,0:T(1,128)S(1)} all-to-all(f32[64,1,16]{2,1,0:T(1,128)S(1)} %broadcast_in_dim.89), channel_id=1, replica_groups=mesh['row_0'=4,'row_1'=4,'col_0'=4,'col_1'=2] {'row_0','row_1','col_0'}, dimensions={0} | all-to-all | bytes 8192 | tf_op jit(solution)/shard_map/all_to_all | solution.py:26
  (204 shorter events, 179.5 us)
Async XLA Ops:
  0.6 14.9 %copy-start = (s32[1,16384]{1,0:T(1,128)S(1)}, s32[1,16384]{1,0:T(1,128)}, u32[]{:S(2)}) copy-start(s32[1,16384]{1,0:T(1,128)} %param.13) | copy-start | bytes 196612
  4.0 47.4 %copy-start.10 = (pred[256]{0:T(512)(128)(4,1)}, pred[256]{0:T(512)(128)(4,1)S(1)}, u32[]{:S(2)}) copy-start(pred[256]{0:T(512)(128)(4,1)S(1)} %iota_compare_fusion.4) | copy-start | bytes 772
  6.1 0.6 copy-start.8
  9.7 19.8 %all-to-all-start = ((bf16[8,64,256]{2,1,0:T(8,128)(2,1)}), bf16[8,64,256]{2,1,0:T(8,128)(2,1)S(1)}, u32[]{:S(2)}, u32[]{:S(2)}) async-start(bf16[8,64,256]{2,1,0:T(8,128)(2,1)} %broadcast_in_dim.74), calls=%async_computation | async-start | bytes 524288 | tf_op jit(solution)/shard_map/all_to_all | solution.py:26
  29.8 13.0 %copy-start.4 = (f32[16,2048]{1,0:T(8,128)S(1)}, f32[16,2048]{1,0:T(8,128)}, u32[]{:S(2)}) copy-start(f32[16,2048]{1,0:T(8,128)} %param.11) | copy-start | bytes 393220
  34.8 21.3 %copy-start.1 = (bf16[64,2048]{1,0:T(8,128)(2,1)S(1)}, bf16[64,2048]{1,0:T(8,128)(2,1)}, u32[]{:S(2)}) copy-start(bf16[64,2048]{1,0:T(8,128)(2,1)} %param.10) | copy-start | bytes 786436
  34.8 37.1 %all-to-all-start.1 = ((bf16[16,64,1024]{2,1,0:T(8,128)(2,1)}), bf16[16,64,1024]{2,1,0:T(8,128)(2,1)S(1)}, u32[]{:S(2)}, u32[]{:S(2)}) async-start(bf16[16,64,1024]{2,1,0:T(8,128)(2,1)} %broadcast_in_dim.75), calls=%async_computation.1 | async-start | bytes 4194304 | tf_op jit(solution)/shard_map/all_to_all | solution.py:26
  72.4 0.6 copy-start.2
  132.0 0.6 copy-start.6
  142.2 16.4 %all-to-all-start.7 = ((f32[64,2,256]{2,1,0:T(2,128)}), f32[64,2,256]{2,1,0:T(2,128)S(1)}, u32[]{:S(2)}, u32[]{:S(2)}) async-start(f32[64,2,256]{2,1,0:T(2,128)} %reduce_sum.238), calls=%async_computation.7 | async-start | bytes 262144 | tf_op jit(solution)/shard_map/all_to_all | solution.py:50
  155.7 23.8 %copy-start.3 = (f32[16,1024]{1,0:T(8,128)S(1)}, f32[16,1024]{1,0:T(8,128)}, u32[]{:S(2)}) copy-start(f32[16,1024]{1,0:T(8,128)} %copy-done.2) | copy-start | bytes 196612
  158.6 7.1 %all-to-all-start.2 = ((f32[2,64,16,128]{3,1,2,0:T(8,128)}), f32[2,64,16,128]{3,1,2,0:T(8,128)S(1)}, u32[]{:S(2)}, u32[]{:S(2)}) async-start(f32[2,64,16,128]{3,1,2,0:T(8,128)} %copy.124), calls=%async_computation.2 | async-start | bytes 2097152 | tf_op jit(solution)/shard_map/all_to_all | solution.py:43
  164.0 30.4 %copy-start.7 = (f32[256]{0:T(256)S(1)}, f32[256]{0:T(256)}, u32[]{:S(2)}) copy-start(f32[256]{0:T(256)} %slice.161) | copy-start | bytes 3076
  166.4 16.7 %all-to-all-start.8 = ((f32[64,2,256]{2,1,0:T(2,128)}), f32[64,2,256]{2,1,0:T(2,128)S(1)}, u32[]{:S(2)}, u32[]{:S(2)}) async-start(f32[64,2,256]{2,1,0:T(2,128)} %broadcast_in_dim.80), calls=%async_computation.8 | async-start | bytes 262144 | tf_op jit(solution)/shard_map/all_to_all | solution.py:26
  188.6 62.0 %copy-start.12 = (s32[2]{0:T(128)S(1)}, s32[2]{0:T(128)}, u32[]{:S(2)}) copy-start(s32[2]{0:T(128)} %iota_multiply_fusion) | copy-start | bytes 28
  188.6 42.9 %all-to-all-start.3 = ((f32[64,16,128]{2,1,0:T(8,128)}), f32[64,16,128]{2,1,0:T(8,128)S(1)}, u32[]{:S(2)}, u32[]{:S(2)}) async-start(f32[64,16,128]{2,1,0:T(8,128)} %copy.126), calls=%async_computation.3 | async-start | bytes 1048576 | tf_op jit(solution)/shard_map/all_to_all | solution.py:50
  232.6 10.3 %all-to-all-start.4 = ((f32[8,1,4112]{2,1,0:T(1,128)}), f32[8,1,4112]{2,1,0:T(1,128)S(1)}, u32[]{:S(2)}, u32[]{:S(2)}) async-start(f32[8,1,4112]{2,1,0:T(1,128)} %broadcast_in_dim.78), calls=%async_computation.4 | async-start | bytes 270336 | tf_op jit(solution)/shard_map/all_to_all | solution.py:26
  243.8 32.6 %all-to-all-start.5 = ((f32[16,1,4112]{2,1,0:T(1,128)}), f32[16,1,4112]{2,1,0:T(1,128)S(1)}, u32[]{:S(2)}, u32[]{:S(2)}) async-start(f32[16,1,4112]{2,1,0:T(1,128)} %broadcast_in_dim.79), calls=%async_computation.5 | async-start | bytes 540672 | tf_op jit(solution)/shard_map/all_to_all | solution.py:26
  278.7 13.3 %all-to-all-start.10 = ((bf16[16,16,128]{2,1,0:T(8,128)(2,1)}), bf16[16,16,128]{2,1,0:T(8,128)(2,1)S(1)}, u32[]{:S(2)}, u32[]{:S(2)}) async-start(bf16[16,16,128]{2,1,0:T(8,128)(2,1)} %broadcast_in_dim.82), calls=%async_computation.10 | async-start | bytes 131072 | tf_op jit(solution)/shard_map/all_to_all | solution.py:26
  295.3 103.8 %copy-start.5 = (f32[16,2048]{1,0:T(8,128)S(1)}, f32[16,2048]{1,0:T(8,128)}, u32[]{:S(2)}) copy-start(f32[16,2048]{1,0:T(8,128)} %param.11) | copy-start | bytes 393220
  295.3 103.8 %copy-start.9 = (s32[256]{0:T(256)S(1)}, s32[256]{0:T(256)}, u32[]{:S(2)}) copy-start(s32[256]{0:T(256)} %copy-done.8) | copy-start | bytes 3076
  295.4 103.8 %copy-start.11 = (pred[256]{0:T(512)(128)(4,1)S(1)}, pred[256]{0:T(512)(128)(4,1)}, u32[]{:S(2)}) copy-start(pred[256]{0:T(512)(128)(4,1)} %copy-done.10) | copy-start | bytes 772
  310.3 14.1 %all-to-all-start.13 = ((f32[64,1,16]{2,1,0:T(1,128)}), f32[64,1,16]{2,1,0:T(1,128)S(1)}, u32[]{:S(2)}, u32[]{:S(2)}) async-start(f32[64,1,16]{2,1,0:T(1,128)} %broadcast_in_dim.84), calls=%async_computation.13 | async-start | bytes 65536 | tf_op jit(solution)/shard_map/all_to_all | solution.py:26
  389.2 9.9 %all-to-all-start.20 = ((f32[8,16,128]{2,1,0:T(8,128)}), f32[8,16,128]{2,1,0:T(8,128)S(1)}, u32[]{:S(2)}, u32[]{:S(2)}) async-start(f32[8,16,128]{2,1,0:T(8,128)} %broadcast_in_dim.90), calls=%async_computation.20 | async-start | bytes 131072 | tf_op jit(solution)/shard_map/all_to_all | solution.py:26
where the time goes:
time: 407 us; the launch traced here: 401 us
  blocking collectives  82.2 us (20%)
  matrix products  75.7 us (19%)
  starting transfers between devices  69.5 us (17%)
  other arithmetic  65.6 us (16%)
  local copies, waits for them, and re-layouts  60.1 us (15%)
  waiting for transfers between devices  41.4 us (10%)
  between operations  6.33 us (2%)
    all_to_all x7, blocking collectives, copy_for_each(): lax.all_to_all(jnp.broadcast_to(array[None], (devices, *array.shape)), ax...  56.2 us
    dot_general x8, matrix products, slab_piece(): part = jnp.dot(weights_bf, kern, preferred_element_type=jnp.float32)  55.7 us
    all_to_all x8, starting transfers between devices, copy_for_each(): lax.all_to_all(jnp.broadcast_to(array[None], (devices, *array.shape)), ax...  51.1 us
    all_to_all x8, waiting for transfers between devices, copy_for_each(): lax.all_to_all(jnp.broadcast_to(array[None], (devices, *array.shape)), ax...  38.8 us
    another operation x6, other arithmetic, on_device(): chol = jnp.linalg.cholesky(inner)  33.9 us
    another operation x4, other arithmetic, solve_inner(): lax.linalg.triangular_solve(chol, middle, left_side=True, lower=True, tra...  21.1 us
    all_to_all x2, blocking collectives, sum_at_owner_2(): lax.all_to_all(parts, axis, split_axis=0, concat_axis=0, tiled=True)  20.6 us
    all_to_all x2, starting transfers between devices, sum_by_axis(): return jnp.sum(lax.all_to_all(own, far, 0, 0, tiled=True), axis=0)  13 us
  transfers between devices with their start and end apart: 11, of which 8 were waited for; matrix products, arithmetic and copies ran while one was open for 26% of the time, Pallas kernels for 0%

commit v1 on v0

v1 whole, which is shorter than its diff:
```python
import math

import jax
import jax.numpy as jnp
from jax import lax
from jax.experimental import pallas as pl
from jax.experimental.pallas import tpu as pltpu
from jax.sharding import Mesh
from jax.sharding import PartitionSpec as P

RANK = 256
ridge = 1.0
AXES = ("row_0", "row_1", "col_0", "col_1")
MESH = pl.DeviceIdType.MESH
HI = lax.Precision.HIGHEST
F32 = jnp.float32
BF16 = jnp.bfloat16
LOG2E = math.log2(math.e)
TAIL = 16


def wrap(value, size):
    return lax.rem(value, size)


class Place:
    def __init__(self):
        self.sizes = tuple(lax.axis_size(a) for a in AXES)
        self.at = tuple(lax.axis_index(a) for a in AXES)
        ny, nz, nx, nc = self.sizes
        self.rows, self.cols = ny * nz, nx * nc
        self.row = self.at[0] * nz + self.at[1]
        self.col = self.at[2] * nc + self.at[3]
        self.device = self.row * self.cols + self.col

        def hops(step, size):
            return min(step, size - step)

        self.row_steps = sorted(
            ((a, b) for a in range(ny) for b in range(nz) if a or b),
            key=lambda s: -(hops(s[0], ny) + hops(s[1], nz)),
        )
        self.col_steps = sorted(
            ((a, b) for a in range(nx) for b in range(nc) if a or b),
            key=lambda s: -(2 * hops(s[0], nx) + s[1]),
        )

    def row_peer(self, step):
        y = wrap(self.at[0] + step[0], self.sizes[0])
        z = wrap(self.at[1] + step[1], self.sizes[1])
        return y * self.sizes[1] + z, (y, z, self.at[2], self.at[3])

    def col_peer(self, step):
        x = wrap(self.at[2] + step[0], self.sizes[2])
        c = wrap(self.at[3] + step[1], self.sizes[3])
        return x * self.sizes[3] + c, (self.at[0], self.at[1], x, c)

    def x_peers(self):
        out = []
        for step in range(1, self.sizes[2]):
            x = wrap(self.at[2] + step, self.sizes[2])
            out.append((x, (self.at[0], self.at[1], x, self.at[3])))
        return out

    def twin(self):
        return self.col_peer((0, 1))[1]

    def row_peers(self):
        return [self.row_peer(s) for s in self.row_steps]

    def col_peers(self):
        return [self.col_peer(s) for s in self.col_steps]

    def row_before(self, k):
        ny, nz = self.sizes[:2]
        steps = sorted(
            ((a, b) for a in range(ny) for b in range(nz) if a or b),
            key=lambda s: (min(s[0], ny - s[0]) + min(s[1], nz - s[1]), s),
        )
        ys = sum(a << (2 * i) for i, (a, _) in enumerate(steps))
        zs = sum(b << (2 * i) for i, (_, b) in enumerate(steps))
        ys, zs = (lax.rem(jnp.right_shift(jnp.int32(v), 2 * (k - 1)), 4) for v in (ys, zs))
        behind = (wrap(self.at[0] + ny - ys, ny), wrap(self.at[1] + nz - zs, nz))
        ahead = (wrap(self.at[0] + ys, ny), wrap(self.at[1] + zs, nz))
        return behind[0] * nz + behind[1], behind + self.at[2:], ahead + self.at[2:]

    def greet(self):
        barrier = pltpu.get_barrier_semaphore()
        for _, peer in self.row_peers() + self.col_peers():
            pl.semaphore_signal(barrier, inc=1, device_id=peer, device_id_type=MESH)

    def enter(self):
        pl.semaphore_wait(pltpu.get_barrier_semaphore(), self.rows + self.cols - 2)


class Links:
    def __init__(self, sends, recvs):
        self.sends, self.recvs, self.used, self.copies = sends, recvs, 0, []

    def start(self, peers, source, target):
        started = []
        for index, peer in peers:
            copy = pltpu.make_async_remote_copy(
                src_ref=source(index),
                dst_ref=target,
                send_sem=self.sends.at[self.used],
                recv_sem=self.recvs.at[self.used],
                device_id=peer,
                device_id_type=MESH,
            )
            copy.start()
            self.used += 1
            started.append(copy)
        self.copies += started
        return started

    def drain(self):
        for copy in self.copies:
            copy.wait_send()


def arrive(copies):
    for copy in copies:
        copy.wait_recv()


def lanes(index, width):
    return pl.ds(pl.multiple_of(index * width, width), width)


def thirds(value):
    high = value.astype(BF16).astype(F32)
    rest = value - high
    middle = rest.astype(BF16).astype(F32)
    return high, middle, (rest - middle).astype(BF16).astype(F32)


def tail_rows(values, first):
    squares = -0.5 * jnp.sum(values * values, axis=0, keepdims=True)
    parts = thirds(squares)
    shape = (TAIL, values.shape[1])
    at = lax.broadcasted_iota(jnp.int32, shape, 0)
    ones = 8 - first
    rows = jnp.where((at >= ones) & (at < ones + 3), 1.0, 0.0)
    for i in range(3):
        rows = jnp.where(at == first + i, jnp.broadcast_to(parts[i], shape), rows)
    return rows


def as_left(block):
    values = block.astype(F32)
    body = values.shape[0] - TAIL
    left = jnp.concatenate([values[:body], values[body + 8 :], values[body : body + 8]], axis=0)
    return left.T


def kernel_of(left, right, scale):
    return jnp.exp2(scale * jnp.dot(left, right, preferred_element_type=F32))


def total(ref):
    value = ref[0].astype(F32)
    for i in range(1, ref.shape[0]):
        value = value + ref[i].astype(F32)
    return value


def inverse_8(rows, lane):
    shape = (8, 128)
    sub = lax.broadcasted_iota(jnp.int32, shape, 0)
    cols = [jnp.broadcast_to(rows[:, lane + j : lane + j + 1], shape) for j in range(8)]
    for k in range(8):
        pivot = 1.0 / jnp.broadcast_to(cols[k][k : k + 1, :], shape)
        here = sub == k
        column = cols[k]
        for j in range(8):
            if j != k:
                factor = jnp.broadcast_to(cols[j][k : k + 1, :], shape) * pivot
                cols[j] = jnp.where(here, factor, cols[j] - column * factor)
        cols[k] = jnp.where(here, pivot, -column * pivot)
    return cols


def sweep_8(rows, b):
    shape = (8, 128)
    rows = list(rows)
    lane = lax.broadcasted_iota(jnp.int32, shape, 1)
    sub = lax.broadcasted_iota(jnp.int32, shape, 0)
    cols = inverse_8(rows[b], 8 * b)
    inside = (lane >= 8 * b) & (lane < 8 * b + 8)
    right = jnp.where(inside, (lane - 8 * b == sub).astype(F32), rows[b])
    new = None
    for j in range(8):
        term = cols[j] * jnp.broadcast_to(right[j : j + 1, :], shape)
        new = term if new is None else new + term
    spread = [jnp.broadcast_to(new[j : j + 1, :], shape) for j in range(8)]
    for i in range(4):
        if i != b:
            acc = None
            for j in range(8):
                at = 8 * b + j
                term = jnp.broadcast_to(rows[i][:, at : at + 1], shape) * spread[j]
                acc = term if acc is None else acc + term
            rows[i] = jnp.where(inside, 0.0, rows[i]) - acc
    rows[b] = new
    return rows


class Sweep:
    def __init__(self, matrix, k):
        self.matrix, self.at = matrix, pl.multiple_of(k * 32, 32)
        size = matrix.shape[0]
        self.rows = matrix[pl.ds(self.at, 32), :]
        block = pltpu.roll(self.rows, lax.rem(size - self.at, size), 1)[:, :128]
        self.small = [block[8 * i : 8 * i + 8, :] for i in range(4)]

    def inner(self, b):
        self.small = sweep_8(self.small, b)

    def finish(self):
        matrix, at, size = self.matrix, self.at, self.matrix.shape[0]
        lane = lax.broadcasted_iota(jnp.int32, (32, size), 1)
        sub = lax.broadcasted_iota(jnp.int32, (32, size), 0)
        wide = lax.broadcasted_iota(jnp.int32, (size, size), 1)
        inv = jnp.concatenate(self.small, axis=0)[:, :32]
        inside = (lane >= at) & (lane < at + 32)
        right = jnp.where(inside, (lane - at == sub).astype(F32), self.rows)
        new = jnp.dot(inv, right, precision=HI, preferred_element_type=F32)
        left = jnp.where(lane < at, -self.rows, self.rows)
        update = lax.dot_general(
            left, new, (((0,), (0,)), ((), ())), precision=HI, preferred_element_type=F32
        )
        matrix[...] = jnp.where((wide >= at) & (wide < at + 32), 0.0, matrix[...]) - update
        matrix[pl.ds(at, 32), :] = new


def step_kernel(points_in, weights_in, targets_in, index_in, weights_out, residual, *scratch):
    (
        points, weights, targets, index,
        piece, vpiece, pin, vin, share, block, marks,
        own_left, col_left, weights_bf, sketch,
        gram_part, gram_in, gram_own, gram_all, inner, inverse,
        part_mine, part_other, part_twin, part_sum, part_in, cut_part, cut_in, tile,
        half_sketch, proj_own, proj_in, proj_sum, proj_row, proj_all, proj_out,
        dots_own, dots_row, dots_sum, dots_col,
        dir_own, dir_all, dir_f32, dir_col, im_part, im_in, moved,
        sends, recvs, loads, mark_s, mark_r, ag_s, ag_r, fw_s, fw_r, rs_s, rs_r, tw_s, tw_r,
    ) = scratch
    me = Place()
    rows, _, group = block.shape
    here = index_in.at[:, lanes(me.row, group)]
    pairs = [(points_in, points), (here, index), (targets_in, targets), (weights_in, weights)]
    taken = [pltpu.make_async_copy(a, b, loads.at[i]) for i, (a, b) in enumerate(pairs)]
    for copy in taken:
        copy.start()
    me.greet()
    links = Links(sends, recvs)
    for copy in taken:
        copy.wait()
    features, owned = points.shape
    count = weights.shape[0]
    width = group // me.cols
    half = group // 2
    span = min(512, owned)
    scale = 4.0 / features * LOG2E
    pieces = [slice(c * span, (c + 1) * span) for c in range(owned // span)]
    my_lanes = lanes(me.col, width)

    local = index[...] - me.device * owned
    own = targets[...] - ridge * weights[...]
    own = [p.astype(BF16) for p in thirds(own)]
    acc = None
    for c, cut in enumerate(pieces):
        at = lax.broadcasted_iota(jnp.int32, (span, group), 0) + c * span
        chosen = jnp.where(at == local, 1.0, 0.0).astype(BF16)
        left = jnp.concatenate([points[:, cut]] + [p[:, cut] for p in own], axis=0)
        some = jnp.dot(left, chosen, preferred_element_type=F32)
        acc = some if acc is None else acc + some
    for c in range(me.cols):
        cut = slice(c * width, (c + 1) * width)
        piece[c] = acc[:features, cut].astype(BF16)
        parts = acc[features:, cut]
        vpiece[c] = parts[:count] + (parts[count : 2 * count] + parts[2 * count :])
    me.enter()
    first = links.start(me.col_peers(), lambda c: piece.at[c], pin.at[me.col])
    pin[me.col] = piece[me.col]
    vin[me.col] = vpiece[me.col]
    for cut in pieces:
        some = points[:, cut].astype(F32)
        left = jnp.concatenate([some, tail_rows(some, 8)], axis=0)
        own_left[cut, :] = left.T.astype(BF16)
    weights_bf[...] = weights[...].astype(BF16)
    arrive(first)
    mine = total(pin)
    mine = jnp.concatenate([mine, tail_rows(mine, 0)], axis=0).astype(BF16)
    share[...] = mine
    block[me.row, :, my_lanes] = mine
    first = links.start(me.col_peers(), lambda c: share, block.at[me.row, :, my_lanes])
    second = links.start(me.col_peers(), lambda c: vpiece.at[c], vin.at[me.col])
    arrive(first)

    def mark_copy(i):
        return pltpu.make_async_remote_copy(
            src_ref=block.at[0, :, pl.ds(0, RANK)],
            dst_ref=marks,
            send_sem=mark_s.at[i],
            recv_sem=mark_r,
            device_id=me.row_peers()[i][1],
            device_id_type=MESH,
        )

    @pl.when(me.row == 0)
    def _():
        for i in range(rows - 1):
            mark_copy(i).start()
        marks[...] = block[0, :, :RANK]

    mine_half = pl.ds(pl.multiple_of(me.at[3] * half, half), half)

    def ahead_copy(k):
        _, _, peer = me.row_before(k)
        return pltpu.make_async_remote_copy(
            src_ref=block.at[me.row, :, mine_half],
            dst_ref=block.at[me.row, :, mine_half],
            send_sem=ag_s.at[k],
            recv_sem=ag_r.at[k],
            device_id=peer,
            device_id_type=MESH,
        )

    def twin_copy(k):
        row, _, _ = me.row_before(k)
        return pltpu.make_async_remote_copy(
            src_ref=block.at[row, :, mine_half],
            dst_ref=block.at[row, :, mine_half],
            send_sem=fw_s.at[k],
            recv_sem=fw_r.at[k],
            device_id=me.twin(),
            device_id_type=MESH,
        )

    def half_copy(k):
        return pltpu.make_async_remote_copy(
            src_ref=part_other.at[k],
            dst_ref=part_twin.at[k],
            send_sem=tw_s.at[k],
            recv_sem=tw_r.at[k],
            device_id=me.twin(),
            device_id_type=MESH,
        )

    def sum_copy(k):
        _, peer, _ = me.row_before(k)
        return pltpu.make_async_remote_copy(
            src_ref=part_sum.at[k],
            dst_ref=part_in.at[me.row],
            send_sem=rs_s.at[k],
            recv_sem=rs_r.at[k],
            device_id=peer,
            device_id_type=MESH,
        )

    def ahead_start(k, carry):
        ahead_copy(k).start()
        return carry

    deep = 5
    lax.fori_loop(1, deep, ahead_start, 0)

    def slab(row, sweep=None):
        right = block[row]
        out = None
        for c, cut in enumerate(pieces):
            if sweep is not None:
                sweep.inner(c)
            kern = kernel_of(own_left[cut, :], right, scale).astype(BF16)
            some = jnp.dot(weights_bf[:, cut], kern, preferred_element_type=F32)
            out = some if out is None else out + some
        return out

    def pass_on(k):
        ahead_copy(k).wait_recv()
        twin_copy(k).start()

    def of_core(value, core):
        odd = [value[:, c * width : (c + 1) * width] for c in range(1, me.cols, 2)]
        even = [value[:, c * width : (c + 1) * width] for c in range(0, me.cols, 2)]
        return jnp.where(core == 0, jnp.concatenate(even, axis=1), jnp.concatenate(odd, axis=1))

    def slab_start(k, row, sweep=None):
        value = slab(row, sweep)
        part_mine[k] = of_core(value, me.at[3])
        part_other[k] = of_core(value, 1 - me.at[3])
        half_copy(k).start()

    def settle(k):
        half_copy(k).wait_recv()
        part_sum[k] = part_mine[k] + part_twin[k]
        sum_copy(k).start()

    def slab_step(k, carry, settles=True, sweeps=None):
        pl.when(k + deep - 1 < rows)(lambda: ahead_copy(k + deep - 1).start())
        pl.when(k + 1 < rows)(lambda: pass_on(k + 1))
        twin_copy(k).wait_recv()
        sweep = None if sweeps is None else Sweep(inverse, k - sweeps)
        slab_start(k, me.row_before(k)[0], sweep)
        if settles:
            settle(k - 1)
        if sweep is not None:
            sweep.finish()
        return carry

    slab_start(0, me.row)
    pass_on(1)
    slab_step(1, 0, settles=False)
    half_copy(0).wait_recv()
    part_in[me.row] = part_mine[0] + part_twin[0]

    @pl.when(me.row != 0)
    def _():
        mark_copy(0).wait_recv()

    marks_left = as_left(marks[...]).astype(BF16)
    sketch[...] = kernel_of(marks_left, block[me.row], scale)
    turned = (((1,), (1,)), ((), ()))
    sk = sketch[...]
    gram = lax.dot_general(sk, sk, turned, precision=HI, preferred_element_type=F32)
    gram_part[...] = gram.reshape(gram_part.shape)
    gram_in[me.row] = gram_part[me.row, me.at[3]]
    third = links.start(
        me.row_peers(), lambda r: gram_part.at[r, me.at[3]], gram_in.at[me.row]
    )
    half_sketch[...] = of_core(sk, me.at[3])
    lax.fori_loop(2, 6, slab_step, 0)
    arrive(third)
    mine = total(gram_in)
    gram_own[...] = mine
    gram_all[me.at[3], me.row] = mine
    third = links.start(me.row_peers(), lambda r: gram_own, gram_all.at[me.at[3], me.row])
    lax.fori_loop(6, 8, slab_step, 0)
    arrive(third)
    its_half = gram_all.at[me.at[3]]
    third = links.start([(0, me.twin())], lambda r: its_half, its_half)
    lax.fori_loop(8, 9, slab_step, 0)
    landmarks = kernel_of(marks_left, marks[...], scale)
    arrive(third)
    gram = jnp.concatenate([gram_all[0], gram_all[1]], axis=1).reshape(inner.shape)
    inner[...] = ridge * landmarks + gram
    inverse[...] = inner[...]
    lax.fori_loop(9, rows, lambda k, carry: slab_step(k, carry, sweeps=9), 0)

    def left_step(row, carry):
        left = as_left(block[row, :, my_lanes])
        col_left[pl.ds(pl.multiple_of(row * width, width), width), :] = left.astype(BF16)
        return carry

    lax.fori_loop(0, rows, left_step, 0)
    settle(rows - 1)
    right = block[me.row]
    sweep = Sweep(inverse, rows - 9)
    for c in range(rows * width // span):
        cut = slice(c * span, (c + 1) * span)
        sweep.inner(c)
        tile[cut, :] = kernel_of(col_left[cut, :], right, scale).astype(BF16)
    sweep.finish()
    arrive(second)

    def sum_wait(k, carry):
        sum_copy(k).wait_recv()
        return carry

    lax.fori_loop(1, rows, sum_wait, 0)
    summed = -total(part_in)
    cuts = [slice(c * width, (c + 1) * width) for c in range(me.cols)]

    def at_share(value, place, places):
        at = lax.broadcasted_iota(jnp.int32, (count, places * width), 1) // width
        return jnp.where(at == place, jnp.concatenate([value] * places, axis=1), 0.0)

    chips = me.sizes[2]
    summed = summed + at_share(total(vin), me.at[2], chips)
    for c in range(chips):
        cut_part[c] = summed[:, c * width : (c + 1) * width]
    cut_in[me.at[2]] = cut_part[me.at[2]]
    each = count // me.cols

    def sum_start(turn, value):
        for c in range(me.cols):
            proj_own[turn, c] = value[c * each : (c + 1) * each]
        proj_in[turn, me.col] = proj_own[turn, me.col]
        return links.start(
            me.col_peers(), lambda c: proj_own.at[turn, c], proj_in.at[turn, me.col]
        )

    def sum_end(turn, copies):
        arrive(copies)
        mine = total(proj_in.at[turn])
        proj_sum[turn] = mine
        proj_row[turn, me.row] = mine
        landing = proj_row.at[turn, me.row]
        arrive(links.start(me.row_peers(), lambda r: proj_sum.at[turn], landing))
        mine = total(proj_row.at[turn])
        proj_all[turn] = mine
        proj_out[turn, me.col] = mine
        landing = proj_out.at[turn, me.col]
        arrive(links.start(me.col_peers(), lambda c: proj_all.at[turn], landing))
        return jnp.concatenate([proj_out[turn, c] for c in range(me.cols)], axis=0)

    def project(vector, marks_of):
        return lax.dot_general(
            vector, marks_of[...], turned, precision=HI, preferred_element_type=F32
        )

    def precondition(vector, projected):
        def product(left, right):
            return jnp.dot(left, right[...], precision=HI, preferred_element_type=F32)

        solved = product(projected, inverse)
        solved = solved + product(projected - product(solved, inner), inverse)
        mine = sketch[:, my_lanes]
        back = jnp.dot(solved, mine, precision=HI, preferred_element_type=F32)
        return (vector - back) / ridge

    def apply(turn, vector):
        rounded = vector.astype(BF16)
        dir_own[turn] = rounded
        dir_all[turn, :, lanes(me.row, width)] = rounded
        landing = dir_all.at[turn, :, lanes(me.row, width)]
        far = links.start(me.row_peers(), lambda r: dir_own.at[turn], landing)
        dir_f32[turn] = vector
        dir_col[turn, :, my_lanes] = vector
        landing = dir_col.at[turn, :, my_lanes]
        near = links.start(me.col_peers(), lambda c: dir_f32.at[turn], landing)
        arrive(far)
        sums = jnp.dot(dir_all[turn], tile[...], preferred_element_type=F32).astype(BF16)
        for c, cut in enumerate(cuts):
            im_part[turn, c] = sums[:, cut]
        im_in[turn, me.col] = im_part[turn, me.col]
        arrive(near)
        return sums.astype(F32) + at_share(ridge * vector, me.col, me.cols)

    def apply_start(turn):
        return links.start(
            me.col_peers(), lambda c: im_part.at[turn, c], im_in.at[turn, me.col]
        )

    def apply_end(turn, copies, vector):
        arrive(copies)
        return total(im_in.at[turn]) + ridge * vector

    lane = lax.broadcasted_iota(jnp.int32, (count, 128), 1)

    def dots(*pairs):
        out = jnp.zeros((count, 128), F32)
        for i, (a, b) in enumerate(pairs):
            out = jnp.where(lane == i, jnp.sum(a * b, axis=1, keepdims=True), out)
        return out

    pad = jnp.zeros((count, 128), F32)
    going = sum_start(0, jnp.concatenate([project(summed, half_sketch), pad], axis=1))
    near = links.start(me.x_peers(), lambda c: cut_part.at[c], cut_in.at[me.at[2]])
    projected = sum_end(0, going)[:, :RANK]
    arrive(near)
    res = total(cut_in)
    direction = precondition(res, projected)
    image_part = apply(0, direction)
    scalars = dots((dir_col[0], image_part)) + dots(
        (jnp.zeros_like(res), res), (res, direction)
    )
    going = sum_start(1, jnp.concatenate([project(image_part, sketch), scalars], axis=1))
    near = apply_start(0)
    packed = sum_end(1, going)
    image = apply_end(0, near, direction)
    curve, old_rz = packed[:, RANK : RANK + 1], packed[:, RANK + 1 : RANK + 2]
    alpha = old_rz / curve
    res = res - alpha * image
    precond = precondition(res, projected - alpha * packed[:, :RANK])
    image_part = apply(1, precond)
    nothing = (jnp.zeros_like(res), res)
    scalars = dots((dir_col[1], image_part), (dir_col[0], image_part)) + dots(
        nothing, nothing, (precond, image), (res, precond)
    )
    dots_own[...] = scalars
    dots_row[me.row] = scalars
    going = links.start(me.row_peers(), lambda r: dots_own, dots_row.at[me.row])
    near = apply_start(1)
    both = [p.astype(BF16) for turn in range(2) for p in thirds(dir_col[turn])]
    both = jnp.concatenate(both, axis=0)
    for c, cut in enumerate(pieces):
        at = lax.broadcasted_iota(jnp.int32, (span, group), 0) + c * span
        chosen = jnp.where(at == local, 1.0, 0.0).astype(BF16)
        got = lax.dot_general(both, chosen, turned, preferred_element_type=F32)
        for turn in range(2):
            base = 3 * count * turn
            low = got[base + count : base + 2 * count] + got[base + 2 * count : base + 3 * count]
            moved[turn, :, cut] = got[base : base + count] + low
    image_2 = apply_end(1, near, precond)
    arrive(going)
    middle = total(dots_row)
    dots_sum[...] = middle
    dots_col[me.col] = middle
    arrive(links.start(me.col_peers(), lambda c: dots_sum, dots_col.at[me.col]))
    summed = total(dots_col)
    own_curve, cross_b, cross_a, fresh = (summed[:, i : i + 1] for i in range(4))
    beta = fresh / old_rz
    last_curve = own_curve + beta * (cross_a + cross_b) + beta * beta * curve
    step = fresh / last_curve
    residual[...] = res - step * (image_2 + beta * image)
    weights_out[...] = weights[...] + ((alpha + step * beta) * moved[0] + step * moved[1])
    links.drain()

    def drain_step(k, carry):
        ahead_copy(k).wait_send()
        twin_copy(k).wait_send()
        sum_copy(k).wait_send()
        half_copy(k).wait_send()
        return carry

    lax.fori_loop(1, rows, drain_step, 0)
    half_copy(0).wait_send()

    @pl.when(me.row == 0)
    def _():
        for i in range(rows - 1):
            mark_copy(i).wait_send()


def on_device(points, weights, targets, block_index):
    features, owned = points.shape
    count = weights.shape[0]
    rows = lax.axis_size("row_0") * lax.axis_size("row_1")
    cols = lax.axis_size("col_0") * lax.axis_size("col_1")
    group = block_index.shape[1] // rows
    width = group // cols
    depth = features + TAIL
    piece = RANK // rows // lax.axis_size("col_1")
    wide = RANK + 128

    def arrays(kind, *shapes):
        return [pltpu.VMEM(shape, kind) for shape in shapes]

    cores = lax.axis_size("col_1")
    chips = cols // cores
    half = group // cores
    each = count // cols
    scratch = [
        *arrays(BF16, (features, owned)),
        *arrays(F32, (count, owned), (count, owned)),
        *arrays(jnp.int32, (1, group)),
        *arrays(BF16, (cols, features, width)),
        *arrays(F32, (cols, count, width)),
        *arrays(BF16, (cols, features, width)),
        *arrays(F32, (cols, count, width)),
        *arrays(BF16, (depth, width), (rows, depth, group), (depth, RANK)),
        *arrays(BF16, (owned, depth), (rows * width, depth), (count, owned)),
        *arrays(F32, (RANK, group)),
        *arrays(F32, (rows, cores, piece, RANK), (rows, piece, RANK), (piece, RANK)),
        *arrays(F32, (cores, rows, piece, RANK), (RANK, RANK), (RANK, RANK)),
        *arrays(F32, *[(rows, count, half)] * 5),
        *arrays(F32, (chips, count, width), (chips, count, width)),
        *arrays(BF16, (rows * width, group)),
        *arrays(F32, (RANK, half)),
        *arrays(F32, (2, cols, each, wide), (2, cols, each, wide), (2, each, wide)),
        *arrays(F32, (2, rows, each, wide), (2, each, wide), (2, cols, each, wide)),
        *arrays(F32, (count, 128), (rows, count, 128)),
        *arrays(F32, (count, 128), (cols, count, 128)),
        *arrays(BF16, (2, count, width), (2, count, rows * width)),
        *arrays(F32, (2, count, width), (2, count, group)),
        *arrays(BF16, (2, cols, count, width), (2, cols, count, width)),
        *arrays(F32, (2, count, owned)),
    ]
    near, far = cols - 1, rows - 1
    copies = 12 * near + 7 * far + chips
    dma = pltpu.SemaphoreType.DMA
    scratch += [dma((copies,)), dma((copies,)), dma((4,)), dma((far,)), dma]
    scratch += [dma((rows,))] * 8
    return tuple(
        pl.pallas_call(
            step_kernel,
            out_shape=[
                jax.ShapeDtypeStruct((count, owned), F32),
                jax.ShapeDtypeStruct((count, width), F32),
            ],
            in_specs=[pl.BlockSpec(memory_space=pl.ANY)] * 4,
            scratch_shapes=scratch,
            compiler_params=pltpu.CompilerParams(
                vmem_limit_bytes=60 * 2**20, collective_id=0, has_side_effects=True
            ),
            name="step",
        )(points, weights, targets, block_index)
    )


def solution(mesh):
    split = Mesh(mesh.devices.reshape(4, 4, 4, 2), AXES)
    spec = P(None, AXES)
    return jax.shard_map(
        on_device,
        mesh=split,
        in_specs=(spec, spec, spec, P()),
        out_specs=(spec, spec),
        check_vma=False,
    )
```

time: 407 us -> 128 us (0.31); the launches traced: 401 us -> 128 us
  Pallas kernels: 0 us -> 125 us
  blocking collectives: 82.2 us -> 0 us
  matrix products: 75.7 us -> 0 us
  starting transfers between devices: 69.5 us -> 0 us
  other arithmetic: 65.6 us -> 0 us
  local copies, waits for them, and re-layouts: 60.1 us -> 2.18 us
  waiting for transfers between devices: 41.4 us -> 0 us
  between operations: 6.33 us -> 0.65 us
    pallas_call x0 -> x1, Pallas kernels: none -> 125 us  [on_device(): pl.pallas_call(step_kernel, out_shape=[jax.ShapeDtypeStruct((count, owned...]
    all_to_all x10 -> x0, blocking collectives: 82.2 us -> none  [the longest x7 56.2 us: copy_for_each(): lax.all_to_all(jnp.broadcast_to(array[None], (devices, *array.shape)), ax...]
    dot_general x19 -> x0, matrix products: 72.9 us -> none  [the longest x8 55.7 us: slab_piece(): part = jnp.dot(weights_bf, kern, preferred_element_type=jnp.float32)]
    all_to_all x11 -> x0, starting transfers between devices: 69.5 us -> none  [the longest x8 51.1 us: copy_for_each(): lax.all_to_all(jnp.broadcast_to(array[None], (devices, *array.shape)), ax...]
    another operation x10 -> x0, other arithmetic: 55 us -> none  [the longest x6 33.9 us: on_device(): chol = jnp.linalg.cholesky(inner)]
    all_to_all x11 -> x0, waiting for transfers between devices: 41.4 us -> none  [the longest x8 38.8 us: copy_for_each(): lax.all_to_all(jnp.broadcast_to(array[None], (devices, *array.shape)), ax...]
    gather x8 -> x0, local copies, waits for them, and re-layouts: 22.9 us -> none  [the longest x1 6.57 us: on_device(): placing = holder % col_count * capacity + rows_at - firsts[holder]]
    broadcast_in_dim x17 -> x0, local copies, waits for them, and re-layouts: 7.95 us -> none  [the longest x15 6.84 us: copy_for_each(): jnp.broadcast_to(array[None], (devices, *array.shape))]
  transfers between devices with their start and end apart: 11 -> 0, of which waited for: 8 -> 0; matrix products, arithmetic and copies ran while one was open for 26% -> 0% of each run, Pallas kernels for 0% -> 0%
where the time goes in v1:
time: 128 us
  Pallas kernels  125 us (98%)
  local copies, waits for them, and re-layouts  2.18 us (2%)
    pallas_call x1, Pallas kernels, on_device(): pl.pallas_call(step_kernel, out_shape=[jax.ShapeDtypeStruct((count, owned...  125 us

profile of v1, /device:TPU:1, one launch (start us, length us, event | category | flops | bytes accessed | tf_op | source)
XLA Modules:
  0.0 127.6 jit_solution(13288294453740074635)
XLA Ops:
  0.6 124.8 %step.1 = (f32[16,2048]{1,0:T(8,128)}, f32[16,128]{1,0:T(8,128)}) custom-call(bf16[64,2048]{1,0:T(8,128)(2,1)} %points_in.1, f32[16,2048]{1,0:T(8,128)} %weights_in.1, f32[16,2048]{1,0:T(8,128)} %targets_in.1, s32[1,16384]{1,0:T(1,128)} %index_in.1), custom_call_target="tpu_custom_call" | custom-call | tf_op jit(solution)/shard_map/step/pallas_call | solution.py:678
  125.4 0.0 copy-start
  125.4 1.6 %copy.8 = f32[16,2048]{1,0:T(8,128)} copy(f32[16,2048]{1,0:T(8,128)} %get-tuple-element.4) | data formatting | bytes 262144
  127.0 0.0 copy-done
  127.0 0.6 copy.9
Async XLA Ops:
  125.4 1.6 %copy-start = (f32[16,128]{1,0:T(8,128)S(1)}, f32[16,128]{1,0:T(8,128)}, u32[]{:S(2)}) copy-start(f32[16,128]{1,0:T(8,128)} %get-tuple-element.5) | copy-start | bytes 24580

commit v2 on v1

--- a/solution.py
+++ b/solution.py
@@ -207,26 +207,30 @@
 
 
 class Sweep:
-    def __init__(self, matrix, k):
-        self.matrix, self.at = matrix, pl.multiple_of(k * 32, 32)
-        size = matrix.shape[0]
-        self.rows = matrix[pl.ds(self.at, 32), :]
-        block = pltpu.roll(self.rows, lax.rem(size - self.at, size), 1)[:, :128]
-        self.small = [block[8 * i : 8 * i + 8, :] for i in range(4)]
+    def __init__(self, matrix, k, keep):
+        self.matrix, self.keep, self.at = matrix, keep, pl.multiple_of(k * 32, 32)
 
     def inner(self, b):
+        if b == 0:
+            size = self.matrix.shape[0]
+            rows = self.matrix[pl.ds(self.at, 32), :]
+            block = pltpu.roll(rows, lax.rem(size - self.at, size), 1)[:, :128]
+            self.small = [block[8 * i : 8 * i + 8, :] for i in range(4)]
         self.small = sweep_8(self.small, b)
+        if b == 3:
+            self.keep[...] = jnp.concatenate(self.small, axis=0)
 
     def finish(self):
         matrix, at, size = self.matrix, self.at, self.matrix.shape[0]
+        rows = matrix[pl.ds(at, 32), :]
         lane = lax.broadcasted_iota(jnp.int32, (32, size), 1)
         sub = lax.broadcasted_iota(jnp.int32, (32, size), 0)
         wide = lax.broadcasted_iota(jnp.int32, (size, size), 1)
-        inv = jnp.concatenate(self.small, axis=0)[:, :32]
+        inv = self.keep[:, :32]
         inside = (lane >= at) & (lane < at + 32)
-        right = jnp.where(inside, (lane - at == sub).astype(F32), self.rows)
+        right = jnp.where(inside, (lane - at == sub).astype(F32), rows)
         new = jnp.dot(inv, right, precision=HI, preferred_element_type=F32)
-        left = jnp.where(lane < at, -self.rows, self.rows)
+        left = jnp.where(lane < at, -rows, rows)
         update = lax.dot_general(
             left, new, (((0,), (0,)), ((), ())), precision=HI, preferred_element_type=F32
         )
@@ -239,11 +243,12 @@
         points, weights, targets, index,
         piece, vpiece, pin, vin, share, block, marks,
         own_left, col_left, weights_bf, sketch,
-        gram_part, gram_in, gram_own, gram_all, inner, inverse,
+        gram_part, gram_in, gram_own, gram_all, inner, inverse, keep,
         part_mine, part_other, part_twin, part_sum, part_in, cut_part, cut_in, tile,
         half_sketch, proj_own, proj_in, proj_sum, proj_row, proj_all, proj_out,
         dots_own, dots_row, dots_sum, dots_col,
-        dir_own, dir_all, dir_f32, dir_col, im_part, im_in, moved,
+        vec_own, vec_all, vec_col, dir_col, im_part, im_in, moved,
+        col_right, col_sketch, pair,
         sends, recvs, loads, mark_s, mark_r, ag_s, ag_r, fw_s, fw_r, rs_s, rs_r, tw_s, tw_r,
     ) = scratch
     me = Place()
@@ -367,15 +372,25 @@
     deep = 5
     lax.fori_loop(1, deep, ahead_start, 0)
 
-    def slab(row, sweep=None):
+    def beside(piece, sweep, last):
+        if piece == 0 and last is not None:
+            last.finish()
+        if piece > 0 and sweep is not None:
+            sweep.inner(piece - 1)
+
+    def slab(row, sweep=None, last=None):
         right = block[row]
         out = None
         for c, cut in enumerate(pieces):
-            if sweep is not None:
-                sweep.inner(c)
+            beside(c, sweep, last)
             kern = kernel_of(own_left[cut, :], right, scale).astype(BF16)
             some = jnp.dot(weights_bf[:, cut], kern, preferred_element_type=F32)
             out = some if out is None else out + some
+        beside(len(pieces), sweep, last)
+        mine = block[row, :, my_lanes]
+        col_right[:, lanes(row, width)] = mine
+        left = as_left(mine)
+        col_left[pl.ds(pl.multiple_of(row * width, width), width), :] = left.astype(BF16)
         return out
 
     def pass_on(k):
@@ -387,8 +402,8 @@
         even = [value[:, c * width : (c + 1) * width] for c in range(0, me.cols, 2)]
         return jnp.where(core == 0, jnp.concatenate(even, axis=1), jnp.concatenate(odd, axis=1))
 
-    def slab_start(k, row, sweep=None):
-        value = slab(row, sweep)
+    def slab_start(k, row, sweep=None, last=None):
+        value = slab(row, sweep, last)
         part_mine[k] = of_core(value, me.at[3])
         part_other[k] = of_core(value, 1 - me.at[3])
         half_copy(k).start()
@@ -398,28 +413,24 @@
         part_sum[k] = part_mine[k] + part_twin[k]
         sum_copy(k).start()
 
-    def slab_step(k, carry, settles=True, sweeps=None):
+    def slab_step(k, carry, settles=True, sweeps=None, ends=False):
         pl.when(k + deep - 1 < rows)(lambda: ahead_copy(k + deep - 1).start())
         pl.when(k + 1 < rows)(lambda: pass_on(k + 1))
         twin_copy(k).wait_recv()
-        sweep = None if sweeps is None else Sweep(inverse, k - sweeps)
-        slab_start(k, me.row_before(k)[0], sweep)
+        sweep = None if sweeps is None else Sweep(inverse, k - sweeps, keep)
+        last = Sweep(inverse, k - sweeps - 1, keep) if ends else None
+        slab_start(k, me.row_before(k)[0], sweep, last)
         if settles:
             settle(k - 1)
-        if sweep is not None:
-            sweep.finish()
         return carry
 
     slab_start(0, me.row)
-    pass_on(1)
-    slab_step(1, 0, settles=False)
-    half_copy(0).wait_recv()
-    part_in[me.row] = part_mine[0] + part_twin[0]
 
     @pl.when(me.row != 0)
     def _():
         mark_copy(0).wait_recv()
 
+    pass_on(1)
     marks_left = as_left(marks[...]).astype(BF16)
     sketch[...] = kernel_of(marks_left, block[me.row], scale)
     turned = (((1,), (1,)), ((), ()))
@@ -431,13 +442,16 @@
         me.row_peers(), lambda r: gram_part.at[r, me.at[3]], gram_in.at[me.row]
     )
     half_sketch[...] = of_core(sk, me.at[3])
-    lax.fori_loop(2, 6, slab_step, 0)
+    slab_step(1, 0, settles=False)
+    half_copy(0).wait_recv()
+    part_in[me.row] = part_mine[0] + part_twin[0]
+    lax.fori_loop(2, 5, slab_step, 0)
     arrive(third)
     mine = total(gram_in)
     gram_own[...] = mine
     gram_all[me.at[3], me.row] = mine
     third = links.start(me.row_peers(), lambda r: gram_own, gram_all.at[me.at[3], me.row])
-    lax.fori_loop(6, 8, slab_step, 0)
+    lax.fori_loop(5, 8, slab_step, 0)
     arrive(third)
     its_half = gram_all.at[me.at[3]]
     third = links.start([(0, me.twin())], lambda r: its_half, its_half)
@@ -447,22 +461,33 @@
     gram = jnp.concatenate([gram_all[0], gram_all[1]], axis=1).reshape(inner.shape)
     inner[...] = ridge * landmarks + gram
     inverse[...] = inner[...]
-    lax.fori_loop(9, rows, lambda k, carry: slab_step(k, carry, sweeps=9), 0)
-
-    def left_step(row, carry):
-        left = as_left(block[row, :, my_lanes])
-        col_left[pl.ds(pl.multiple_of(row * width, width), width), :] = left.astype(BF16)
-        return carry
-
-    lax.fori_loop(0, rows, left_step, 0)
-    settle(rows - 1)
+    slab_step(9, 0, sweeps=9)
+    lax.fori_loop(10, rows, lambda k, carry: slab_step(k, carry, sweeps=9, ends=True), 0)
+
     right = block[me.row]
-    sweep = Sweep(inverse, rows - 9)
-    for c in range(rows * width // span):
+    sweep, last = Sweep(inverse, rows - 9, keep), Sweep(inverse, rows - 10, keep)
+    parts = rows * width // span
+    for c in range(parts):
         cut = slice(c * span, (c + 1) * span)
-        sweep.inner(c)
+        beside(c, sweep, last)
         tile[cut, :] = kernel_of(col_left[cut, :], right, scale).astype(BF16)
+        if c == 0:
+            settle(rows - 1)
+    beside(parts, sweep, last)
     sweep.finish()
+
+    parts = thirds(kernel_of(marks_left, col_right[...], scale))
+    for i, some in enumerate(parts):
+        col_sketch[i * RANK : (i + 1) * RANK, :] = some.astype(BF16)
+    step = group // 4
+    for c in range(4):
+        cut = slice(c * step, (c + 1) * step)
+        got = jnp.dot(col_sketch[...], tile[:, cut], preferred_element_type=F32)
+        got = got[:RANK] + (got[RANK : 2 * RANK] + got[2 * RANK :])
+        for i, some in enumerate(thirds(got)):
+            pair[i, :, cut] = some.astype(BF16)
+    for i, some in enumerate(thirds(sketch[...])):
+        pair[i, :, group:] = some.astype(BF16)
     arrive(second)
 
     def sum_wait(k, carry):
@@ -476,6 +501,10 @@
     def at_share(value, place, places):
         at = lax.broadcasted_iota(jnp.int32, (count, places * width), 1) // width
         return jnp.where(at == place, jnp.concatenate([value] * places, axis=1), 0.0)
+
+    def of_share(value):
+        at = lax.broadcasted_iota(jnp.int32, (count, group), 1) // width
+        return jnp.where(at == me.col, value, 0.0)
 
     chips = me.sizes[2]
     summed = summed + at_share(total(vin), me.at[2], chips)
@@ -492,18 +521,24 @@
             me.col_peers(), lambda c: proj_own.at[turn, c], proj_in.at[turn, me.col]
         )
 
-    def sum_end(turn, copies):
+    def sum_rows(turn, copies):
         arrive(copies)
         mine = total(proj_in.at[turn])
         proj_sum[turn] = mine
         proj_row[turn, me.row] = mine
         landing = proj_row.at[turn, me.row]
-        arrive(links.start(me.row_peers(), lambda r: proj_sum.at[turn], landing))
+        return links.start(me.row_peers(), lambda r: proj_sum.at[turn], landing)
+
+    def sum_back(turn, copies):
+        arrive(copies)
         mine = total(proj_row.at[turn])
         proj_all[turn] = mine
         proj_out[turn, me.col] = mine
         landing = proj_out.at[turn, me.col]
-        arrive(links.start(me.col_peers(), lambda c: proj_all.at[turn], landing))
+        return links.start(me.col_peers(), lambda c: proj_all.at[turn], landing)
+
+    def sum_end(turn, copies):
+        arrive(copies)
         return jnp.concatenate([proj_out[turn, c] for c in range(me.cols)], axis=0)
 
     def project(vector, marks_of):
@@ -511,42 +546,58 @@
             vector, marks_of[...], turned, precision=HI, preferred_element_type=F32
         )
 
-    def precondition(vector, projected):
+    def project_pair(vector):
+        parts = [p.astype(BF16) for p in thirds(vector)]
+        out = []
+        for i in range(3):
+            left = jnp.concatenate(parts[: 3 - i], axis=0)
+            right = pair[i, :, group:]
+            got = lax.dot_general(left, right, turned, preferred_element_type=F32)
+            out.append([got[j * count : (j + 1) * count] for j in range(3 - i)])
+        return out[0][0] + ((out[0][1] + out[1][0]) + (out[0][2] + (out[1][1] + out[2][0])))
+
+    def solve(projected):
         def product(left, right):
             return jnp.dot(left, right[...], precision=HI, preferred_element_type=F32)
 
         solved = product(projected, inverse)
-        solved = solved + product(projected - product(solved, inner), inverse)
-        mine = sketch[:, my_lanes]
-        back = jnp.dot(solved, mine, precision=HI, preferred_element_type=F32)
-        return (vector - back) / ridge
-
-    def apply(turn, vector):
-        rounded = vector.astype(BF16)
-        dir_own[turn] = rounded
-        dir_all[turn, :, lanes(me.row, width)] = rounded
-        landing = dir_all.at[turn, :, lanes(me.row, width)]
-        far = links.start(me.row_peers(), lambda r: dir_own.at[turn], landing)
-        dir_f32[turn] = vector
-        dir_col[turn, :, my_lanes] = vector
-        landing = dir_col.at[turn, :, my_lanes]
-        near = links.start(me.col_peers(), lambda c: dir_f32.at[turn], landing)
-        arrive(far)
-        sums = jnp.dot(dir_all[turn], tile[...], preferred_element_type=F32).astype(BF16)
+        return solved + product(projected - product(solved, inner), inverse)
+
+    def times_pair(vector):
+        parts = [p.astype(BF16) for p in thirds(vector)]
+        out = []
+        for i in range(3):
+            left = jnp.concatenate(parts[: 3 - i], axis=0)
+            got = jnp.dot(left, pair[i], preferred_element_type=F32)
+            out.append([got[j * count : (j + 1) * count] for j in range(3 - i)])
+        got = out[0][0] + ((out[0][1] + out[1][0]) + (out[0][2] + (out[1][1] + out[2][0])))
+        return got[:, :group], got[:, group:]
+
+    def spread(turn, value):
+        vec_own[turn] = value
+        vec_all[turn, me.row] = value
+        far = links.start(me.row_peers(), lambda r: vec_own.at[turn], vec_all.at[turn, me.row])
+        vec_col[turn, :, my_lanes] = value
+        landing = vec_col.at[turn, :, my_lanes]
+        return far, links.start(me.col_peers(), lambda c: vec_own.at[turn], landing)
+
+    def block_times(turn):
+        value = jnp.concatenate([vec_all[turn, r] for r in range(rows)], axis=1)
+        value = jnp.concatenate([p.astype(BF16) for p in thirds(value)], axis=0)
+        got = jnp.dot(value, tile[...], preferred_element_type=F32)
+        return got[:count] + (got[count : 2 * count] + got[2 * count :])
+
+    def image_start(turn, value):
         for c, cut in enumerate(cuts):
-            im_part[turn, c] = sums[:, cut]
+            im_part[turn, c] = value[:, cut]
         im_in[turn, me.col] = im_part[turn, me.col]
-        arrive(near)
-        return sums.astype(F32) + at_share(ridge * vector, me.col, me.cols)
-
-    def apply_start(turn):
         return links.start(
             me.col_peers(), lambda c: im_part.at[turn, c], im_in.at[turn, me.col]
         )
 
-    def apply_end(turn, copies, vector):
+    def image_end(turn, copies):
         arrive(copies)
-        return total(im_in.at[turn]) + ridge * vector
+        return total(im_in.at[turn])
 
     lane = lax.broadcasted_iota(jnp.int32, (count, 128), 1)
 
@@ -559,31 +610,49 @@
     pad = jnp.zeros((count, 128), F32)
     going = sum_start(0, jnp.concatenate([project(summed, half_sketch), pad], axis=1))
     near = links.start(me.x_peers(), lambda c: cut_part.at[c], cut_in.at[me.at[2]])
-    projected = sum_end(0, going)[:, :RANK]
+    going = sum_rows(0, going)
     arrive(near)
     res = total(cut_in)
-    direction = precondition(res, projected)
-    image_part = apply(0, direction)
-    scalars = dots((dir_col[0], image_part)) + dots(
-        (jnp.zeros_like(res), res), (res, direction)
-    )
-    going = sum_start(1, jnp.concatenate([project(image_part, sketch), scalars], axis=1))
-    near = apply_start(0)
+    far, near = spread(0, res)
+    going = sum_back(0, going)
+    arrive(far)
+    block_res = block_times(0)
+    arrive(near)
+    res_row = vec_col[0]
+    projected = sum_end(0, going)[:, :RANK]
+    image_part, back = times_pair(solve(projected))
+    direction = (res_row - back) / ridge
+    dir_col[0] = direction
+    image_part = (block_res - image_part) / ridge + of_share(ridge * direction)
+    scalars = dots((direction, image_part), (of_share(direction), res_row))
+    going = sum_start(1, jnp.concatenate([project_pair(image_part), scalars], axis=1))
+    near = image_start(0, image_part)
+    going = sum_rows(1, going)
+    image = image_end(0, near)
+    far, near = spread(1, image)
+    going = sum_back(1, going)
+    arrive(far)
+    block_image = block_times(1)
+    arrive(near)
+    image_row = vec_col[1]
     packed = sum_end(1, going)
-    image = apply_end(0, near, direction)
     curve, old_rz = packed[:, RANK : RANK + 1], packed[:, RANK + 1 : RANK + 2]
     alpha = old_rz / curve
     res = res - alpha * image
-    precond = precondition(res, projected - alpha * packed[:, :RANK])
-    image_part = apply(1, precond)
-    nothing = (jnp.zeros_like(res), res)
-    scalars = dots((dir_col[1], image_part), (dir_col[0], image_part)) + dots(
-        nothing, nothing, (precond, image), (res, precond)
+    res_row = res_row - alpha * image_row
+    image_part, back = times_pair(solve(projected - alpha * packed[:, :RANK]))
+    precond = (res_row - back) / ridge
+    dir_col[1] = precond
+    image_part = (block_res - alpha * block_image - image_part) / ridge
+    image_part = image_part + of_share(ridge * precond)
+    mine = of_share(precond)
+    scalars = dots(
+        (precond, image_part), (direction, image_part), (mine, image_row), (mine, res_row)
     )
     dots_own[...] = scalars
     dots_row[me.row] = scalars
     going = links.start(me.row_peers(), lambda r: dots_own, dots_row.at[me.row])
-    near = apply_start(1)
+    near = image_start(1, image_part)
     both = [p.astype(BF16) for turn in range(2) for p in thirds(dir_col[turn])]
     both = jnp.concatenate(both, axis=0)
     for c, cut in enumerate(pieces):
@@ -594,7 +663,7 @@
             base = 3 * count * turn
             low = got[base + count : base + 2 * count] + got[base + 2 * count : base + 3 * count]
             moved[turn, :, cut] = got[base : base + count] + low
-    image_2 = apply_end(1, near, precond)
+    image_2 = image_end(1, near)
     arrive(going)
     middle = total(dots_row)
     dots_sum[...] = middle
@@ -655,7 +724,7 @@
         *arrays(BF16, (owned, depth), (rows * width, depth), (count, owned)),
         *arrays(F32, (RANK, group)),
         *arrays(F32, (rows, cores, piece, RANK), (rows, piece, RANK), (piece, RANK)),
-        *arrays(F32, (cores, rows, piece, RANK), (RANK, RANK), (RANK, RANK)),
+        *arrays(F32, (cores, rows, piece, RANK), (RANK, RANK), (RANK, RANK), (32, 128)),
         *arrays(F32, *[(rows, count, half)] * 5),
         *arrays(F32, (chips, count, width), (chips, count, width)),
         *arrays(BF16, (rows * width, group)),
@@ -664,10 +733,12 @@
         *arrays(F32, (2, rows, each, wide), (2, each, wide), (2, cols, each, wide)),
         *arrays(F32, (count, 128), (rows, count, 128)),
         *arrays(F32, (count, 128), (cols, count, 128)),
-        *arrays(BF16, (2, count, width), (2, count, rows * width)),
-        *arrays(F32, (2, count, width), (2, count, group)),
-        *arrays(BF16, (2, cols, count, width), (2, cols, count, width)),
+        *arrays(F32, (2, count, width), (2, rows, count, width)),
+        *arrays(F32, (2, count, group), (2, count, group)),
+        *arrays(F32, (2, cols, count, width), (2, cols, count, width)),
         *arrays(F32, (2, count, owned)),
+        *arrays(BF16, (depth, rows * width), (3 * RANK, rows * width)),
+        *arrays(BF16, (3, RANK, 2 * group)),
     ]
     near, far = cols - 1, rows - 1
     copies = 12 * near + 7 * far + chips

time: 128 us -> 116 us (0.906)
  Pallas kernels: 125 us -> 113 us
    pallas_call x1, Pallas kernels: 125 us -> 113 us  [on_device(): pl.pallas_call(step_kernel, out_shape=[jax.ShapeDtypeStruct((count, owned...]
where the time goes in v2:
time: 116 us
  Pallas kernels  113 us (97%)
  local copies, waits for them, and re-layouts  2.18 us (2%)
    pallas_call x1, Pallas kernels, on_device(): pl.pallas_call(step_kernel, out_shape=[jax.ShapeDtypeStruct((count, owned...  113 us

profile of v2, /device:TPU:1, one launch (start us, length us, event | category | flops | bytes accessed | tf_op | source)
XLA Modules:
  0.0 115.9 jit_solution(15413622934814449178)
XLA Ops:
  0.6 113.1 %step.1 = (f32[16,2048]{1,0:T(8,128)}, f32[16,128]{1,0:T(8,128)}) custom-call(bf16[64,2048]{1,0:T(8,128)(2,1)} %points_in.1, f32[16,2048]{1,0:T(8,128)} %weights_in.1, f32[16,2048]{1,0:T(8,128)} %targets_in.1, s32[1,16384]{1,0:T(1,128)} %index_in.1), custom_call_target="tpu_custom_call" | custom-call | tf_op jit(solution)/shard_map/step/pallas_call | solution.py:749
  113.7 0.0 copy-start
  113.7 1.6 %copy.8 = f32[16,2048]{1,0:T(8,128)} copy(f32[16,2048]{1,0:T(8,128)} %get-tuple-element.4) | data formatting | bytes 262144
  115.3 0.0 copy-done
  115.3 0.6 copy.9
Async XLA Ops:
  113.7 1.6 %copy-start = (f32[16,128]{1,0:T(8,128)S(1)}, f32[16,128]{1,0:T(8,128)}, u32[]{:S(2)}) copy-start(f32[16,128]{1,0:T(8,128)} %get-tuple-element.5) | copy-start | bytes 24580

commit v3 on v2

--- a/solution.py
+++ b/solution.py
@@ -95,33 +95,34 @@
 
 class Links:
     def __init__(self, sends, recvs):
-        self.sends, self.recvs, self.used, self.copies = sends, recvs, 0, []
-
-    def start(self, peers, source, target):
-        started = []
+        self.sends, self.recvs, self.wholes = sends, recvs, []
+
+    def start(self, peers, source, target, whole):
+        at = len(self.wholes)
+        self.wholes.append(whole)
         for index, peer in peers:
-            copy = pltpu.make_async_remote_copy(
+            pltpu.make_async_remote_copy(
                 src_ref=source(index),
                 dst_ref=target,
-                send_sem=self.sends.at[self.used],
-                recv_sem=self.recvs.at[self.used],
+                send_sem=self.sends.at[at],
+                recv_sem=self.recvs.at[at],
                 device_id=peer,
                 device_id_type=MESH,
-            )
-            copy.start()
-            self.used += 1
-            started.append(copy)
-        self.copies += started
-        return started
+            ).start()
+        return whole, self.recvs.at[at]
 
     def drain(self):
-        for copy in self.copies:
-            copy.wait_send()
-
-
-def arrive(copies):
-    for copy in copies:
-        copy.wait_recv()
+        for at, whole in enumerate(self.wholes):
+            arrive((whole, self.sends.at[at]))
+
+
+def arrive(exchange):
+    whole, semaphore = exchange
+    pltpu.make_async_copy(whole, whole, semaphore).wait()
+
+
+def head(ref, length):
+    return ref.at[pl.ds(0, length)]
 
 
 def lanes(index, width):
@@ -260,6 +261,7 @@
         copy.start()
     me.greet()
     links = Links(sends, recvs)
+    near_count, far_count = me.cols - 1, rows - 1
     for copy in taken:
         copy.wait()
     features, owned = points.shape
@@ -287,7 +289,9 @@
         parts = acc[features:, cut]
         vpiece[c] = parts[:count] + (parts[count : 2 * count] + parts[2 * count :])
     me.enter()
-    first = links.start(me.col_peers(), lambda c: piece.at[c], pin.at[me.col])
+    first = links.start(
+        me.col_peers(), lambda c: piece.at[c], pin.at[me.col], head(pin, near_count)
+    )
     pin[me.col] = piece[me.col]
     vin[me.col] = vpiece[me.col]
     for cut in pieces:
@@ -300,15 +304,18 @@
     mine = jnp.concatenate([mine, tail_rows(mine, 0)], axis=0).astype(BF16)
     share[...] = mine
     block[me.row, :, my_lanes] = mine
-    first = links.start(me.col_peers(), lambda c: share, block.at[me.row, :, my_lanes])
-    second = links.start(me.col_peers(), lambda c: vpiece.at[c], vin.at[me.col])
+    most = block.at[me.row, :, pl.ds(0, near_count * width)]
+    first = links.start(me.col_peers(), lambda c: share, block.at[me.row, :, my_lanes], most)
+    second = links.start(
+        me.col_peers(), lambda c: vpiece.at[c], vin.at[me.col], head(vin, near_count)
+    )
     arrive(first)
 
     def mark_copy(i):
         return pltpu.make_async_remote_copy(
             src_ref=block.at[0, :, pl.ds(0, RANK)],
             dst_ref=marks,
-            send_sem=mark_s.at[i],
+            send_sem=mark_s,
             recv_sem=mark_r,
             device_id=me.row_peers()[i][1],
             device_id_type=MESH,
@@ -327,7 +334,7 @@
         return pltpu.make_async_remote_copy(
             src_ref=block.at[me.row, :, mine_half],
             dst_ref=block.at[me.row, :, mine_half],
-            send_sem=ag_s.at[k],
+            send_sem=ag_s,
             recv_sem=ag_r.at[k],
             device_id=peer,
             device_id_type=MESH,
@@ -338,7 +345,7 @@
         return pltpu.make_async_remote_copy(
             src_ref=block.at[row, :, mine_half],
             dst_ref=block.at[row, :, mine_half],
-            send_sem=fw_s.at[k],
+            send_sem=fw_s,
             recv_sem=fw_r.at[k],
             device_id=me.twin(),
             device_id_type=MESH,
@@ -348,7 +355,7 @@
         return pltpu.make_async_remote_copy(
             src_ref=part_other.at[k],
             dst_ref=part_twin.at[k],
-            send_sem=tw_s.at[k],
+            send_sem=tw_s,
             recv_sem=tw_r.at[k],
             device_id=me.twin(),
             device_id_type=MESH,
@@ -359,8 +366,8 @@
         return pltpu.make_async_remote_copy(
             src_ref=part_sum.at[k],
             dst_ref=part_in.at[me.row],
-            send_sem=rs_s.at[k],
-            recv_sem=rs_r.at[k],
+            send_sem=rs_s,
+            recv_sem=rs_r,
             device_id=peer,
             device_id_type=MESH,
         )
@@ -426,11 +433,15 @@
 
     slab_start(0, me.row)
 
+    pass_on(1)
+    slab_step(1, 0, settles=False)
+    half_copy(0).wait_recv()
+    part_in[me.row] = part_mine[0] + part_twin[0]
+
     @pl.when(me.row != 0)
     def _():
         mark_copy(0).wait_recv()
 
-    pass_on(1)
     marks_left = as_left(marks[...]).astype(BF16)
     sketch[...] = kernel_of(marks_left, block[me.row], scale)
     turned = (((1,), (1,)), ((), ()))
@@ -439,22 +450,24 @@
     gram_part[...] = gram.reshape(gram_part.shape)
     gram_in[me.row] = gram_part[me.row, me.at[3]]
     third = links.start(
-        me.row_peers(), lambda r: gram_part.at[r, me.at[3]], gram_in.at[me.row]
+        me.row_peers(),
+        lambda r: gram_part.at[r, me.at[3]],
+        gram_in.at[me.row],
+        head(gram_in, far_count),
     )
     half_sketch[...] = of_core(sk, me.at[3])
-    slab_step(1, 0, settles=False)
-    half_copy(0).wait_recv()
-    part_in[me.row] = part_mine[0] + part_twin[0]
     lax.fori_loop(2, 5, slab_step, 0)
     arrive(third)
     mine = total(gram_in)
     gram_own[...] = mine
     gram_all[me.at[3], me.row] = mine
-    third = links.start(me.row_peers(), lambda r: gram_own, gram_all.at[me.at[3], me.row])
+    its_half = gram_all.at[me.at[3]]
+    third = links.start(
+        me.row_peers(), lambda r: gram_own, its_half.at[me.row], head(its_half, far_count)
+    )
     lax.fori_loop(5, 8, slab_step, 0)
     arrive(third)
-    its_half = gram_all.at[me.at[3]]
-    third = links.start([(0, me.twin())], lambda r: its_half, its_half)
+    third = links.start([(0, me.twin())], lambda r: its_half, its_half, its_half)
     lax.fori_loop(8, 9, slab_step, 0)
     landmarks = kernel_of(marks_left, marks[...], scale)
     arrive(third)
@@ -490,11 +503,7 @@
         pair[i, :, group:] = some.astype(BF16)
     arrive(second)
 
-    def sum_wait(k, carry):
-        sum_copy(k).wait_recv()
-        return carry
-
-    lax.fori_loop(1, rows, sum_wait, 0)
+    arrive((head(part_in, far_count), rs_r))
     summed = -total(part_in)
     cuts = [slice(c * width, (c + 1) * width) for c in range(me.cols)]
 
@@ -518,7 +527,10 @@
             proj_own[turn, c] = value[c * each : (c + 1) * each]
         proj_in[turn, me.col] = proj_own[turn, me.col]
         return links.start(
-            me.col_peers(), lambda c: proj_own.at[turn, c], proj_in.at[turn, me.col]
+            me.col_peers(),
+            lambda c: proj_own.at[turn, c],
+            proj_in.at[turn, me.col],
+            head(proj_in.at[turn], near_count),
         )
 
     def sum_rows(turn, copies):
@@ -526,16 +538,16 @@
         mine = total(proj_in.at[turn])
         proj_sum[turn] = mine
         proj_row[turn, me.row] = mine
-        landing = proj_row.at[turn, me.row]
-        return links.start(me.row_peers(), lambda r: proj_sum.at[turn], landing)
+        landing, whole = proj_row.at[turn, me.row], head(proj_row.at[turn], far_count)
+        return links.start(me.row_peers(), lambda r: proj_sum.at[turn], landing, whole)
 
     def sum_back(turn, copies):
         arrive(copies)
         mine = total(proj_row.at[turn])
         proj_all[turn] = mine
         proj_out[turn, me.col] = mine
-        landing = proj_out.at[turn, me.col]
-        return links.start(me.col_peers(), lambda c: proj_all.at[turn], landing)
+        landing, whole = proj_out.at[turn, me.col], head(proj_out.at[turn], near_count)
+        return links.start(me.col_peers(), lambda c: proj_all.at[turn], landing, whole)
 
     def sum_end(turn, copies):
         arrive(copies)
@@ -576,10 +588,12 @@
     def spread(turn, value):
         vec_own[turn] = value
         vec_all[turn, me.row] = value
-        far = links.start(me.row_peers(), lambda r: vec_own.at[turn], vec_all.at[turn, me.row])
+        landing, whole = vec_all.at[turn, me.row], head(vec_all.at[turn], far_count)
+        far = links.start(me.row_peers(), lambda r: vec_own.at[turn], landing, whole)
         vec_col[turn, :, my_lanes] = value
         landing = vec_col.at[turn, :, my_lanes]
-        return far, links.start(me.col_peers(), lambda c: vec_own.at[turn], landing)
+        whole = vec_col.at[turn, :, pl.ds(0, near_count * width)]
+        return far, links.start(me.col_peers(), lambda c: vec_own.at[turn], landing, whole)
 
     def block_times(turn):
         value = jnp.concatenate([vec_all[turn, r] for r in range(rows)], axis=1)
@@ -592,7 +606,10 @@
             im_part[turn, c] = value[:, cut]
         im_in[turn, me.col] = im_part[turn, me.col]
         return links.start(
-            me.col_peers(), lambda c: im_part.at[turn, c], im_in.at[turn, me.col]
+            me.col_peers(),
+            lambda c: im_part.at[turn, c],
+            im_in.at[turn, me.col],
+            head(im_in.at[turn], near_count),
         )
 
     def image_end(turn, copies):
@@ -609,7 +626,9 @@
 
     pad = jnp.zeros((count, 128), F32)
     going = sum_start(0, jnp.concatenate([project(summed, half_sketch), pad], axis=1))
-    near = links.start(me.x_peers(), lambda c: cut_part.at[c], cut_in.at[me.at[2]])
+    near = links.start(
+        me.x_peers(), lambda c: cut_part.at[c], cut_in.at[me.at[2]], head(cut_in, chips - 1)
+    )
     going = sum_rows(0, going)
     arrive(near)
     res = total(cut_in)
@@ -651,7 +670,9 @@
     )
     dots_own[...] = scalars
     dots_row[me.row] = scalars
-    going = links.start(me.row_peers(), lambda r: dots_own, dots_row.at[me.row])
+    going = links.start(
+        me.row_peers(), lambda r: dots_own, dots_row.at[me.row], head(dots_row, far_count)
+    )
     near = image_start(1, image_part)
     both = [p.astype(BF16) for turn in range(2) for p in thirds(dir_col[turn])]
     both = jnp.concatenate(both, axis=0)
@@ -668,7 +689,11 @@
     middle = total(dots_row)
     dots_sum[...] = middle
     dots_col[me.col] = middle
-    arrive(links.start(me.col_peers(), lambda c: dots_sum, dots_col.at[me.col]))
+    arrive(
+        links.start(
+            me.col_peers(), lambda c: dots_sum, dots_col.at[me.col], head(dots_col, near_count)
+        )
+    )
     summed = total(dots_col)
     own_curve, cross_b, cross_a, fresh = (summed[:, i : i + 1] for i in range(4))
     beta = fresh / old_rz
@@ -677,21 +702,14 @@
     residual[...] = res - step * (image_2 + beta * image)
     weights_out[...] = weights[...] + ((alpha + step * beta) * moved[0] + step * moved[1])
     links.drain()
-
-    def drain_step(k, carry):
-        ahead_copy(k).wait_send()
-        twin_copy(k).wait_send()
-        sum_copy(k).wait_send()
-        half_copy(k).wait_send()
-        return carry
-
-    lax.fori_loop(1, rows, drain_step, 0)
-    half_copy(0).wait_send()
+    arrive((block.at[pl.ds(0, far_count), :, mine_half], ag_s))
+    arrive((block.at[pl.ds(0, far_count), :, mine_half], fw_s))
+    arrive((head(part_in, far_count), rs_s))
+    arrive((part_in, tw_s))
 
     @pl.when(me.row == 0)
     def _():
-        for i in range(rows - 1):
-            mark_copy(i).wait_send()
+        arrive((block.at[pl.ds(0, far_count), :, pl.ds(0, RANK)], mark_s))
 
 
 def on_device(points, weights, targets, block_index):
@@ -740,11 +758,9 @@
         *arrays(BF16, (depth, rows * width), (3 * RANK, rows * width)),
         *arrays(BF16, (3, RANK, 2 * group)),
     ]
-    near, far = cols - 1, rows - 1
-    copies = 12 * near + 7 * far + chips
     dma = pltpu.SemaphoreType.DMA
-    scratch += [dma((copies,)), dma((copies,)), dma((4,)), dma((far,)), dma]
-    scratch += [dma((rows,))] * 8
+    scratch += [dma((21,)), dma((21,)), dma((4,)), dma, dma]
+    scratch += [dma, dma((rows,)), dma, dma((rows,)), dma, dma, dma, dma((rows,))]
     return tuple(
         pl.pallas_call(
             step_kernel,

time: 116 us -> 109 us (0.940)
  Pallas kernels: 113 us -> 106 us
    pallas_call x1, Pallas kernels: 113 us -> 106 us  [on_device(): pl.pallas_call(step_kernel, out_shape=[jax.ShapeDtypeStruct((count, owned...]
where the time goes in v3:
time: 109 us; the launch traced here: 108 us
  Pallas kernels  106 us (97%)
  local copies, waits for them, and re-layouts  2.18 us (2%)
    pallas_call x1, Pallas kernels, on_device(): pl.pallas_call(step_kernel, out_shape=[jax.ShapeDtypeStruct((count, owned...  106 us

profile of v3, /device:TPU:1, one launch (start us, length us, event | category | flops | bytes accessed | tf_op | source)
XLA Modules:
  0.0 108.4 jit_solution(15210188317600295017)
XLA Ops:
  0.6 105.6 %step.1 = (f32[16,2048]{1,0:T(8,128)}, f32[16,128]{1,0:T(8,128)}) custom-call(bf16[64,2048]{1,0:T(8,128)(2,1)} %points_in.1, f32[16,2048]{1,0:T(8,128)} %weights_in.1, f32[16,2048]{1,0:T(8,128)} %targets_in.1, s32[1,16384]{1,0:T(1,128)} %index_in.1), custom_call_target="tpu_custom_call" | custom-call | tf_op jit(solution)/shard_map/step/pallas_call | solution.py:765
  106.2 0.0 copy-start
  106.2 1.6 %copy.8 = f32[16,2048]{1,0:T(8,128)} copy(f32[16,2048]{1,0:T(8,128)} %get-tuple-element.4) | data formatting | bytes 262144
  107.8 0.0 copy-done
  107.8 0.6 copy.9
Async XLA Ops:
  106.2 1.6 %copy-start = (f32[16,128]{1,0:T(8,128)S(1)}, f32[16,128]{1,0:T(8,128)}, u32[]{:S(2)}) copy-start(f32[16,128]{1,0:T(8,128)} %get-tuple-element.5) | copy-start | bytes 24580

commit v4 on v3

--- a/solution.py
+++ b/solution.py
@@ -239,7 +239,12 @@
         matrix[pl.ds(at, 32), :] = new
 
 
-def step_kernel(points_in, weights_in, targets_in, index_in, weights_out, residual, *scratch):
+def end_kernel(weights, change, residual, weights_out, residual_out):
+    weights_out[...] = weights[...] + change[...]
+    residual_out[...] = residual[...]
+
+
+def step_kernel(points_in, weights_in, targets_in, index_in, change, residual, *scratch):
     (
         points, weights, targets, index,
         piece, vpiece, pin, vin, share, block, marks,
@@ -484,23 +489,24 @@
         cut = slice(c * span, (c + 1) * span)
         beside(c, sweep, last)
         tile[cut, :] = kernel_of(col_left[cut, :], right, scale).astype(BF16)
-        if c == 0:
+        if c == 1:
             settle(rows - 1)
     beside(parts, sweep, last)
-    sweep.finish()
 
     parts = thirds(kernel_of(marks_left, col_right[...], scale))
     for i, some in enumerate(parts):
         col_sketch[i * RANK : (i + 1) * RANK, :] = some.astype(BF16)
-    step = group // 4
-    for c in range(4):
-        cut = slice(c * step, (c + 1) * step)
+    quarter = group // 4
+
+    def pair_piece(c):
+        cut = slice(c * quarter, (c + 1) * quarter)
         got = jnp.dot(col_sketch[...], tile[:, cut], preferred_element_type=F32)
         got = got[:RANK] + (got[RANK : 2 * RANK] + got[2 * RANK :])
         for i, some in enumerate(thirds(got)):
             pair[i, :, cut] = some.astype(BF16)
-    for i, some in enumerate(thirds(sketch[...])):
-        pair[i, :, group:] = some.astype(BF16)
+
+    pair_piece(0)
+    pair_piece(1)
     arrive(second)
 
     arrive((head(part_in, far_count), rs_r))
@@ -629,6 +635,11 @@
     near = links.start(
         me.x_peers(), lambda c: cut_part.at[c], cut_in.at[me.at[2]], head(cut_in, chips - 1)
     )
+    sweep.finish()
+    pair_piece(2)
+    pair_piece(3)
+    for i, some in enumerate(thirds(sketch[...])):
+        pair[i, :, group:] = some.astype(BF16)
     going = sum_rows(0, going)
     arrive(near)
     res = total(cut_in)
@@ -700,7 +711,7 @@
     last_curve = own_curve + beta * (cross_a + cross_b) + beta * beta * curve
     step = fresh / last_curve
     residual[...] = res - step * (image_2 + beta * image)
-    weights_out[...] = weights[...] + ((alpha + step * beta) * moved[0] + step * moved[1])
+    change[...] = (alpha + step * beta) * moved[0] + step * moved[1]
     links.drain()
     arrive((block.at[pl.ds(0, far_count), :, mine_half], ag_s))
     arrive((block.at[pl.ds(0, far_count), :, mine_half], fw_s))
@@ -761,20 +772,22 @@
     dma = pltpu.SemaphoreType.DMA
     scratch += [dma((21,)), dma((21,)), dma((4,)), dma, dma]
     scratch += [dma, dma((rows,)), dma, dma((rows,)), dma, dma, dma, dma((rows,))]
+    outs = [
+        jax.ShapeDtypeStruct((count, owned), F32),
+        jax.ShapeDtypeStruct((count, width), F32),
+    ]
+    change, residual = pl.pallas_call(
+        step_kernel,
+        out_shape=outs,
+        in_specs=[pl.BlockSpec(memory_space=pl.ANY)] * 4,
+        scratch_shapes=scratch,
+        compiler_params=pltpu.CompilerParams(
+            vmem_limit_bytes=60 * 2**20, collective_id=0, has_side_effects=True
+        ),
+        name="step",
+    )(points, weights, targets, block_index)
     return tuple(
-        pl.pallas_call(
-            step_kernel,
-            out_shape=[
-                jax.ShapeDtypeStruct((count, owned), F32),
-                jax.ShapeDtypeStruct((count, width), F32),
-            ],
-            in_specs=[pl.BlockSpec(memory_space=pl.ANY)] * 4,
-            scratch_shapes=scratch,
-            compiler_params=pltpu.CompilerParams(
-                vmem_limit_bytes=60 * 2**20, collective_id=0, has_side_effects=True
-            ),
-            name="step",
-        )(points, weights, targets, block_index)
+        pl.pallas_call(end_kernel, out_shape=outs, name="end")(weights, change, residual)
     )
 
 

time: 109 us -> 107 us (0.982)
  local copies, waits for them, and re-layouts: 2.18 us -> 0 us
    unnamed x4 -> x0, local copies, waits for them, and re-layouts: 2.18 us -> none
    pallas_call x1 -> x2, Pallas kernels: 106 us -> 106 us  [the longest x1 105 us: on_device(): pl.pallas_call(step_kernel, out_shape=outs, in_specs=[pl.BlockSpec(memory...]
where the time goes in v4:
time: 107 us
  Pallas kernels  106 us (99%)
    pallas_call x1, Pallas kernels, on_device(): pl.pallas_call(step_kernel, out_shape=outs, in_specs=[pl.BlockSpec(memory...  105 us

profile of v4, /device:TPU:1, one launch (start us, length us, event | category | flops | bytes accessed | tf_op | source)
XLA Modules:
  0.0 107.0 jit_solution(2041648679173749771)
XLA Ops:
  0.6 104.7 %step.1 = (f32[16,2048]{1,0:T(8,128)}, f32[16,128]{1,0:T(8,128)}) custom-call(bf16[64,2048]{1,0:T(8,128)(2,1)} %points_in.1, f32[16,2048]{1,0:T(8,128)} %weights.1, f32[16,2048]{1,0:T(8,128)} %targets_in.1, s32[1,16384]{1,0:T(1,128)} %index_in.1), custom_call_target="tpu_custom_call" | custom-call | tf_op jit(solution)/shard_map/step/pallas_call | solution.py:779
  105.3 1.6 %end.1 = (f32[16,2048]{1,0:T(8,128)}, f32[16,128]{1,0:T(8,128)}) custom-call(f32[16,2048]{1,0:T(8,128)} %weights.1, f32[16,2048]{1,0:T(8,128)} %get-tuple-element.4.change, f32[16,128]{1,0:T(8,128)} %get-tuple-element.5.residual), custom_call_target="tpu_custom_call" | custom-call | tf_op jit(solution)/shard_map/end/pallas_call | solution.py:790

commit v5 on v4

--- a/solution.py
+++ b/solution.py
@@ -679,6 +679,7 @@
     scalars = dots(
         (precond, image_part), (direction, image_part), (mine, image_row), (mine, res_row)
     )
+    scalars = jnp.concatenate([scalars.T[:8], jnp.zeros((8, 128 - count), F32)], axis=1)
     dots_own[...] = scalars
     dots_row[me.row] = scalars
     going = links.start(
@@ -705,7 +706,7 @@
             me.col_peers(), lambda c: dots_sum, dots_col.at[me.col], head(dots_col, near_count)
         )
     )
-    summed = total(dots_col)
+    summed = total(dots_col).T[:count]
     own_curve, cross_b, cross_a, fresh = (summed[:, i : i + 1] for i in range(4))
     beta = fresh / old_rz
     last_curve = own_curve + beta * (cross_a + cross_b) + beta * beta * curve
@@ -760,8 +761,8 @@
         *arrays(F32, (RANK, half)),
         *arrays(F32, (2, cols, each, wide), (2, cols, each, wide), (2, each, wide)),
         *arrays(F32, (2, rows, each, wide), (2, each, wide), (2, cols, each, wide)),
-        *arrays(F32, (count, 128), (rows, count, 128)),
-        *arrays(F32, (count, 128), (cols, count, 128)),
+        *arrays(F32, (8, 128), (rows, 8, 128)),
+        *arrays(F32, (8, 128), (cols, 8, 128)),
         *arrays(F32, (2, count, width), (2, rows, count, width)),
         *arrays(F32, (2, count, group), (2, count, group)),
         *arrays(F32, (2, cols, count, width), (2, cols, count, width)),

time: 107 us -> 107 us (level)
  no operation moved by 1% of the time
where the time goes in v5:
time: 107 us
  Pallas kernels  106 us (99%)
    pallas_call x1, Pallas kernels, on_device(): pl.pallas_call(step_kernel, out_shape=outs, in_specs=[pl.BlockSpec(memory...  105 us

profile of v5, /device:TPU:1, one launch (start us, length us, event | category | flops | bytes accessed | tf_op | source)
XLA Modules:
  0.0 106.9 jit_solution(9136516343014829335)
XLA Ops:
  0.6 104.7 %step.1 = (f32[16,2048]{1,0:T(8,128)}, f32[16,128]{1,0:T(8,128)}) custom-call(bf16[64,2048]{1,0:T(8,128)(2,1)} %points_in.1, f32[16,2048]{1,0:T(8,128)} %weights.1, f32[16,2048]{1,0:T(8,128)} %targets_in.1, s32[1,16384]{1,0:T(1,128)} %index_in.1), custom_call_target="tpu_custom_call" | custom-call | tf_op jit(solution)/shard_map/step/pallas_call | solution.py:780
  105.3 1.6 %end.1 = (f32[16,2048]{1,0:T(8,128)}, f32[16,128]{1,0:T(8,128)}) custom-call(f32[16,2048]{1,0:T(8,128)} %weights.1, f32[16,2048]{1,0:T(8,128)} %get-tuple-element.4.change, f32[16,128]{1,0:T(8,128)} %get-tuple-element.5.residual), custom_call_target="tpu_custom_call" | custom-call | tf_op jit(solution)/shard_map/end/pallas_call | solution.py:791
